TPU v7x, 32 devices: a whole 2x2x4 slice. The times are simulated.
32 devices in a mesh: tm: 4 (over x, core), cohort: 8 (over z, y).
Axes of the slice: x: 2, y: 2, z: 4, core: 2. Of those that a mesh axis runs over, the one named last changes fastest.
Arguments:
- transition: float32 [32, 16, 256, 256], P('tm', 'cohort'), may hold values from 0 to 1, as said below
- entry: int32 [16], P('cohort'), may hold values from 0 to 31, as said below
- share: float32 [16], P('cohort'), may hold values from 0.1 to 1
Outputs:
- cumulative: float32 [32, 16, 256, 256], P('tm', 'cohort')
- pooled: float32 [32, 256, 256], P('tm', 'cohort')
Inputs may be any that keep to these rules, and one draw needn't show every extreme that they name: `entry`: month numbers within the window; some group enters at month 0 and some at the window's last month. `transition`: each row of every monthly matrix is nonnegative and sums to one, with a diagonal entry of at least 0.7.
All inputs are finite; a program needn't handle non-finite values.
Results may differ from a plain program's by a relative error of at most 0.0001.
Values sent between devices are 32-bit elements; how exact they have to be, the bound alone decides.
No kernel may reach another device: no remote copies, remote signals or barrier semaphores. Data moves between devices by JAX's collectives and lax.ppermute only.
A program may use at most 64 MiB of HBM per device.

v0:
```python
import functools

import jax
import jax.numpy as jnp
from jax import lax
from jax.experimental import pallas as pl
from jax.experimental.pallas import tpu as pltpu
from jax.sharding import PartitionSpec as P


kernel_weights = (1.0 / 16, 2.0 / 16, 3.0 / 16, 4.0 / 16, 3.0 / 16, 2.0 / 16, 1.0 / 16)
REACH = 3
VMEM = pl.BlockSpec(memory_space=pltpu.VMEM)
SMEM = pl.BlockSpec(memory_space=pltpu.SMEM)
ANY = pl.BlockSpec(memory_space=pl.ANY)
HBM = pl.BlockSpec(memory_space=pltpu.HBM)
f32, bf16 = jnp.float32, jnp.bfloat16
shaped = jax.ShapeDtypeStruct


def split(x):
    hi = x.astype(bf16)
    return hi, (x - hi.astype(f32)).astype(bf16)


def product(a, b):
    dot = functools.partial(jnp.dot, preferred_element_type=f32)
    return dot(a[0], b[0]) + (dot(a[0], b[1]) + dot(a[1], b[0]))


def put(pair, hi_ref, lo_ref, at):
    hi_ref[at], lo_ref[at] = pair


def unit_rows(rows, states, start):
    row = lax.broadcasted_iota(jnp.int32, (rows, states), 0) + start
    return (row == lax.broadcasted_iota(jnp.int32, (rows, states), 1)).astype(f32)


def inverse_weight(month, months_all):
    value = jnp.float32(1.0)
    for edge in range(months_all):
        inside = [
            kernel_weights[k + REACH]
            for k in range(-REACH, REACH + 1)
            if 0 <= edge + k < months_all
        ]
        if len(inside) < len(kernel_weights):
            value = jnp.where(month == edge, jnp.float32(1.0 / sum(inside)), value)
    return value


def sides(months, odd):
    wait = range(months - REACH, months) if odd else range(REACH)
    return list(wait), [month for month in range(months) if month not in wait]


def outer_taps(months, odd, month):
    taps = []
    for offset in range(-REACH, REACH + 1):
        at = month + offset
        if odd and at >= months:
            taps.append((kernel_weights[offset + REACH], at - months))
        if not odd and at < 0:
            taps.append((kernel_weights[offset + REACH], at + REACH))
    return taps


def cut_kernel(outside, group, raw_ref, out_ref, sem):
    late = (lax.axis_index("tm") % 2 == 1) == outside
    start = jnp.where(late, raw_ref.shape[0] - REACH, 0)
    source = raw_ref.at[pl.ds(start, REACH), pl.ds(group, out_ref.shape[1])]
    copy = pltpu.make_async_copy(source, out_ref, sem)
    copy.start()
    copy.wait()


def early_kernel(months_all, *refs):
    raw_ref, inner_ref, entry_ref, share_ref = refs[:4]
    months, groups, states = raw_ref.shape[:3]
    open_refs, hi_refs, lo_refs = (refs[4 + k * groups : 4 + (k + 1) * groups] for k in range(3))
    gate_refs = refs[4 + 3 * groups : 4 + 4 * groups]
    total_ref, part_ref, done_hi, done_lo = refs[4 + 4 * groups :]
    line = lax.axis_index("tm")
    first = line * months
    step = 32

    def finished(value, month, group, start):
        value = value * inverse_weight(first + month, months_all)
        unit = unit_rows(value.shape[0], states, start)
        return jnp.where(first + month >= entry_ref[group], value, unit)

    def run(odd):
        wait, done = sides(months, odd)
        for group in range(groups):
            part_ref[group] = jnp.full((8, states), share_ref[group], f32)
            for k, month in enumerate(wait):
                gate = inverse_weight(first + month, months_all)
                gate = jnp.where(first + month >= entry_ref[group], gate, jnp.float32(0.0))
                gate_refs[group][k] = jnp.full((8, states), gate, f32)

            @pl.loop(0, states // step)
            def _(chunk):
                start = pl.multiple_of(chunk * step, step)
                rows = pl.ds(start, step)
                own = [raw_ref[month, group, rows] for month in range(months)]
                near = [inner_ref[k, group, rows] for k in range(REACH)]
                line_up = near + own if odd else own + near
                base = REACH if odd else 0
                for month in range(months):
                    value = None
                    for offset in range(-REACH, REACH + 1):
                        at = base + month + offset
                        if 0 <= at < len(line_up):
                            term = kernel_weights[offset + REACH] * line_up[at]
                            value = term if value is None else value + term
                    if month in wait:
                        open_refs[group][wait.index(month), rows] = value
                    else:
                        at = done.index(month)
                        pair = split(finished(value, month, group, start))
                        done_hi[at, group, rows], done_lo[at, group, rows] = pair

        last = [(done_hi[0, group], done_lo[0, group]) for group in range(groups)]
        for group in range(groups):
            put(last[group], hi_refs[group], lo_refs[group], 0)
        for at in range(1, len(done)):
            for group in range(groups):
                month = (done_hi[at, group], done_lo[at, group])
                last[group] = split(product(last[group], month))
                put(last[group], hi_refs[group], lo_refs[group], at)
        return wait, last

    @pl.when(line % 2 == 0)
    def _():
        wait, _ = run(False)

        @pl.when(line == 0)
        def _():
            for group in range(groups):
                parts = [
                    split(finished(open_refs[group][k], month, group, 0))
                    for k, month in enumerate(wait)
                ]
                head = parts[0]
                for part in parts[1:]:
                    head = split(product(head, part))
                tail = (hi_refs[group][months - REACH - 1],
                        lo_refs[group][months - REACH - 1])
                total_ref[group] = product(head, tail)

    @pl.when(line % 2 == 1)
    def _():
        run(True)


def lead_kernel(*refs):
    before_ref = refs[0]
    groups = before_ref.shape[0]
    hi_refs, lo_refs, out_hi, out_lo = (refs[1 + k * groups : 1 + (k + 1) * groups] for k in range(4))
    second = lax.axis_index("tm") == 1

    @pl.when(second)
    def _():
        before = [split(before_ref[group]) for group in range(groups)]
        for at in range(hi_refs[0].shape[0]):
            for group in range(groups):
                month = (hi_refs[group][at], lo_refs[group][at])
                put(split(product(before[group], month)), out_hi[group], out_lo[group], at)

    @pl.when(jnp.logical_not(second))
    def _():
        for group in range(groups):
            out_hi[group][...] = hi_refs[group][...]
            out_lo[group][...] = lo_refs[group][...]


def closed(odd, open_ref, outer_ref, gate_ref, months):
    states = open_ref.shape[1]
    unit = unit_rows(states, states, 0)
    parts = []
    for k, month in enumerate(sides(months, odd)[0]):
        value = open_ref[k]
        for weight, at in outer_taps(months, odd, month):
            value = value + weight * outer_ref[at, 0]
        gate = gate_ref[k, 0:1, :]
        parts.append(split(jnp.where(gate > 0.0, value * gate, unit)))
    return parts


def close_odd_kernel(open_ref, outer_ref, run_hi, run_lo, gate_ref, hi_ref, lo_ref, total_ref):
    months = hi_ref.shape[0]
    begun = months - REACH

    @pl.when(lax.axis_index("tm") % 2 == 1)
    def _():
        parts = closed(True, open_ref, outer_ref, gate_ref, months)
        last = (run_hi[begun - 1], run_lo[begun - 1])
        for at in range(REACH):
            value = product(last, parts[at])
            last = split(value)
            put(last, hi_ref, lo_ref, begun + at)
        total_ref[...] = value


def close_even_kernel(open_ref, outer_ref, run_hi, run_lo, gate_ref, _hi, _lo, hi_ref, lo_ref):
    months = hi_ref.shape[0]
    begun = months - REACH

    @pl.when(lax.axis_index("tm") % 2 == 0)
    def _():
        parts = closed(False, open_ref, outer_ref, gate_ref, months)
        last = parts[0]
        put(last, hi_ref, lo_ref, 0)
        for at in range(1, REACH):
            last = split(product(last, parts[at]))
            put(last, hi_ref, lo_ref, at)
        for at in reversed(range(begun)):
            value = product(last, (run_hi[at], run_lo[at]))
            put(split(value), hi_ref, lo_ref, at + REACH)

    @pl.when(lax.axis_index("tm") % 2 == 1)
    def _():
        hi_ref[:begun] = run_hi[...]
        lo_ref[:begun] = run_lo[...]


def cross_kernel(carry_ref, hi_ref, lo_ref, out_ref):
    last = hi_ref.shape[0] - 1
    out_ref[...] = product(split(carry_ref[...]), (hi_ref[last], lo_ref[last]))


def place_of(order, place):
    steps = len(order)
    return sum(order[s] for s in range(steps) if place >> (steps - 1 - s) & 1)


def halving_orders(count):
    bits = [1 << s for s in range(count.bit_length() - 1)]
    other = bits[:]
    if len(bits) > 1:
        other[0], other[1] = other[1], other[0]
    return bits, other


def apply_kernel(orders, groups, start, begin, *refs):
    if begin:
        firsts, seconds = refs[:groups], refs[groups : 2 * groups]
        refs = refs[2 * groups :]
    else:
        carry_hi, carry_lo = refs[:2]
        refs = refs[2:]
    hi_refs, lo_refs = refs[:groups], refs[groups : 2 * groups]
    share_ref, cum_ref, keep_ref, send_ref = refs[2 * groups : 2 * groups + 4]
    refs = refs[2 * groups + 4 :]
    if begin:
        carry_hi, carry_lo = refs[:2]
        refs = refs[2:]
    (mix,) = refs
    months, _, states = cum_ref.shape[:3]
    line = lax.axis_index("tm")
    me = lax.axis_index("cohort")
    rows = keep_ref.shape[2]
    half = keep_ref.shape[0]

    if begin:

        @pl.when(line < 2)
        def _():
            for group in range(groups):
                put(split(unit_rows(states, states, 0)), carry_hi, carry_lo, group)

        @pl.when(jnp.logical_and(line >= 2, line % 2 == 0))
        def _():
            for group in range(groups):
                put(split(firsts[group][...]), carry_hi, carry_lo, group)

        @pl.when(jnp.logical_and(line >= 2, line % 2 == 1))
        def _():
            for group in range(groups):
                put(split(seconds[group][...]), carry_hi, carry_lo, group)

    carry = [(carry_hi[group], carry_lo[group]) for group in range(groups)]
    for at in range(months):
        mixed = None
        for group in range(groups):
            month = (hi_refs[group][start + at], lo_refs[group][start + at])
            value = product(carry[group], month)
            cum_ref[at, group] = value
            term = share_ref[group, 0:1, :] * value
            mixed = term if mixed is None else mixed + term
        mix[at] = mixed
    for place in range(2 * half):
        away = jnp.where(line % 2 == 0, place_of(orders[0], place), place_of(orders[1], place))
        block = pl.ds(pl.multiple_of((me ^ away) * rows, 8), rows)
        out = keep_ref if place < half else send_ref
        for at in range(months):
            out[place % half, at] = mix[at, block, :]


def store_kernel(*refs):
    *parts, out_ref, sems = refs
    copies, at = [], 0
    for k, part in enumerate(parts):
        months = part.shape[0]
        copies.append(pltpu.make_async_copy(part, out_ref.at[pl.ds(at, months)], sems.at[k]))
        at += months
    for copy in copies:
        copy.start()
    for copy in copies:
        copy.wait()


def halve_kernel(keep_ref, come_ref, out_keep_ref, out_send_ref):
    half = out_keep_ref.shape[0]
    out_keep_ref[...] = keep_ref[:half] + come_ref[:half]
    out_send_ref[...] = keep_ref[half:] + come_ref[half:]


def end_kernel(*refs):
    *parts, out_ref = refs
    at = 0
    for keep_ref, come_ref in zip(parts[::2], parts[1::2]):
        months = keep_ref.shape[1]
        out_ref[at : at + months] = keep_ref[0] + come_ref[0]
        at += months


def call(kernel, out_shape, in_specs, out_specs, flops, touched, mib=24, **more):
    def run(*args):
        return pl.pallas_call(
            kernel,
            out_shape=out_shape,
            in_specs=in_specs,
            out_specs=out_specs,
            compiler_params=pltpu.CompilerParams(vmem_limit_bytes=mib << 20),
            cost_estimate=pl.CostEstimate(
                flops=int(flops), bytes_accessed=int(touched), transcendentals=0
            ),
            **more,
        )(*args)

    return run


def month_chunks(months):
    counts = [months * 3 // 8, months * 3 // 8, months - 2 * (months * 3 // 8)]
    ends = [sum(counts[: k + 1]) for k in range(len(counts))]
    return [(end - count, end) for end, count in zip(ends, counts)]


def on_device(mesh, transition, entry, share):
    return pipeline(mesh, transition, entry, share)


def pipeline(mesh, transition, entry, share):
    source = pltpu.with_memory_space_constraint(transition, pltpu.HBM)
    months, groups, states = transition.shape[:3]
    lines, cohorts = mesh.shape["tm"], mesh.shape["cohort"]
    months_all = months * lines
    block = (states, states)
    flops = 6 * states**3
    size = 4 * states**2
    line = lax.axis_index("tm")
    rest = months - REACH

    def cut(outside, group, count):
        return call(
            functools.partial(cut_kernel, outside, group),
            shaped((REACH, count) + block, f32),
            [HBM],
            VMEM,
            0,
            2 * REACH * count * size,
            scratch_shapes=[pltpu.SemaphoreType.DMA],
        )(source)

    hops = [(i, i + 1) for i in range(1, lines - 1, 2)]
    cores = [(i, i + 1) for i in range(0, lines - 1, 2)]
    both_ways = lambda pairs: pairs + [(b, a) for a, b in pairs]
    outer = []
    for group in range(groups):
        piece = cut(True, group, 1)
        if True:
            both = lax.ppermute(piece, "tm", both_ways(hops))
            outer.append((both, both))
        else:
            down = lax.ppermute(piece, "tm", [(b, a) for a, b in hops])
            outer.append((down, lax.ppermute(piece, "tm", hops)))
    inner = lax.ppermute(cut(False, 0, groups), "tm", both_ways(cores))

    halves = [shaped((rest,) + block, bf16)] * groups
    early = call(
        functools.partial(early_kernel, months_all),
        tuple(
            [shaped((REACH,) + block, f32)] * groups
            + halves
            + halves
            + [shaped((REACH, 8, states), f32)] * groups
            + [shaped((groups,) + block, f32), shaped((groups, 8, states), f32)]
        ),
        [VMEM, VMEM, SMEM, SMEM],
        tuple([VMEM] * (4 * groups + 2)),
        flops * groups * (rest + 2),
        size * groups * 3 * months,
        scratch_shapes=[pltpu.VMEM((rest, groups) + block, bf16)] * 2,
    )(transition, inner, entry, share)
    opened, run_hi, run_lo, gates = (early[k * groups : (k + 1) * groups] for k in range(4))
    first_total, parts = early[4 * groups :]
    ahead = lax.ppermute(first_total, "tm", [(0, 1)])
    led = call(
        lead_kernel,
        tuple(halves + halves),
        [VMEM] * (1 + 2 * groups),
        tuple([VMEM] * (2 * groups)),
        flops * groups * rest,
        size * groups * rest * 2,
    )(ahead, *run_hi, *run_lo)
    run_hi, run_lo = led[:groups], led[groups:]

    all_months = shaped((months,) + block, bf16)
    hi, lo, first, second = [], [], [], []
    for group in range(groups):
        given = (run_hi[group], run_lo[group], gates[group])
        odd_hi, odd_lo, handed = call(
            close_odd_kernel,
            (all_months, all_months, shaped(block, f32)),
            [VMEM] * 5,
            (VMEM, VMEM, VMEM),
            flops * REACH,
            size * months * 2,
        )(opened[group], outer[group][0], *given)
        hi_all, lo_all = call(
            close_even_kernel,
            (all_months, all_months),
            [VMEM] * 7,
            (VMEM, VMEM),
            flops * months,
            size * months * 2,
            input_output_aliases={5: 0, 6: 1},
        )(opened[group], outer[group][1], *given, odd_hi, odd_lo)
        hi.append(hi_all)
        lo.append(lo_all)
        first.append(jnp.zeros_like(handed) if not hops else None)
        second.append(first[-1])

        def cross(carry):
            return call(cross_kernel, shaped(block, f32), [VMEM] * 3, VMEM, flops, 4 * size)(
                carry, hi_all, lo_all
            )

        for hop, (source, target) in enumerate(hops):
            if hop:
                handed = cross(second[-1])
            one = lax.ppermute(handed, "tm", [(source, target)])
            two = cross(one)
            two = lax.ppermute(two, "tm", [(target, target + 1)])
            if hop:
                here = line // 2 == hop + 1
                one, two = jnp.where(here, one, first[-1]), jnp.where(here, two, second[-1])
            first[-1], second[-1] = one, two

    orders = halving_orders(cohorts)
    steps = len(orders[0])
    rows = states // cohorts
    carry, cumulative, sums = None, [], []
    for chunk, (start, stop) in enumerate(month_chunks(months)):
        count = stop - start
        part = shaped((cohorts // 2, count, rows, states), f32)
        begin = chunk == 0
        outs = [shaped((count, groups) + block, f32), part, part]
        if begin:
            args = (*first, *second)
            outs += [shaped((groups,) + block, bf16)] * 2
        else:
            args = carry
        made = call(
            functools.partial(apply_kernel, orders, groups, start, begin),
            tuple(outs),
            [VMEM] * (len(args) + 2 * groups + 1),
            tuple([VMEM] * len(outs)),
            flops * groups * count,
            size * groups * count * 3,
            scratch_shapes=[pltpu.VMEM((count,) + block, f32)],
        )(*args, *hi, *lo, parts)
        cumulative.append(made[0])
        sums.append(made[1:3])
        if begin:
            carry = tuple(made[3:])
    cumulative = call(
        store_kernel,
        shaped(transition.shape, f32),
        [VMEM] * len(cumulative),
        ANY,
        0,
        2 * months * groups * size,
        scratch_shapes=[pltpu.SemaphoreType.DMA((len(cumulative),))],
    )(*cumulative)

    ends = []
    for keep, send in sums:
        for step in range(steps):
            pairs = [
                (at * cohorts + c, at * cohorts + (c ^ orders[at % 2][step]))
                for at in range(lines)
                for c in range(cohorts)
            ]
            come = lax.ppermute(send, ("tm", "cohort"), pairs)
            if step < steps - 1:
                part = shaped((keep.shape[0] // 2,) + keep.shape[1:], f32)
                keep, send = call(
                    halve_kernel,
                    (part, part),
                    [VMEM, VMEM],
                    (VMEM, VMEM),
                    keep.size,
                    12 * keep.size,
                )(keep, come)
        ends += [keep, come]
    pooled = call(
        end_kernel,
        shaped((months, rows, states), f32),
        [VMEM] * len(ends),
        VMEM,
        months * rows * states,
        12 * months * rows * states,
    )(*ends)
    return cumulative, pooled


def solution(mesh):
    placed = (P("tm", "cohort", None, None), P("cohort"), P("cohort"))
    return jax.shard_map(
        functools.partial(on_device, mesh),
        mesh=mesh,
        in_specs=placed,
        out_specs=(P("tm", "cohort", None, None), P("tm", "cohort", None)),
        check_vma=False,
    )
```

profile of v0, /device:TPU:2, one launch (start us, length us, event | category | flops | bytes accessed | tf_op | source)
XLA Modules:
  0.0 70.6 jit_solution(6284269262596035178)
XLA Ops:
  0.6 1.4 %shard_map.50 = f32[3,2,256,256]{3,2,1,0:T(8,128)S(1)} custom-call(f32[8,2,256,256]{3,2,1,0:T(8,128)} %raw_ref.5), custom_call_target="tpu_custom_call" | custom-call | bytes 3145728 | tf_op jit(solution)/shard_map/pallas_call | solution.py:331
  2.1 1.2 %shard_map.52 = f32[3,1,256,256]{3,2,1,0:T(8,128)S(1)} custom-call(f32[8,2,256,256]{3,2,1,0:T(8,128)} %raw_ref.5), custom_call_target="tpu_custom_call" | custom-call | bytes 1572864 | tf_op jit(solution)/shard_map/pallas_call | solution.py:331
  3.4 2.2 %collective-permute-start.1 = (f32[3,1,256,256]{3,2,1,0:T(8,128)S(1)}, f32[3,1,256,256]{3,2,1,0:T(8,128)S(1)}, u32[]{:S(2)}, u32[]{:S(2)}) collective-permute-start(f32[3,1,256,256]{3,2,1,0:T(8,128)S(1)} %shard_map.52), channel_id=1, source_target_pairs={{8,16},{16,8},{9,17},{17,9},{10,18},{18,10},{11,19},{19,11},{12,20... | collective-permute-start | bytes 2359304 | tf_op jit(solution)/shard_map/ppermute | solution.py:385
  5.5 1.2 %shard_map.55 = f32[3,1,256,256]{3,2,1,0:T(8,128)S(1)} custom-call(f32[8,2,256,256]{3,2,1,0:T(8,128)} %raw_ref.5), custom_call_target="tpu_custom_call" | custom-call | bytes 1572864 | tf_op jit(solution)/shard_map/pallas_call | solution.py:331
  6.7 3.6 %collective-permute-start.4 = (f32[3,1,256,256]{3,2,1,0:T(8,128)S(1)}, f32[3,1,256,256]{3,2,1,0:T(8,128)S(1)}, u32[]{:S(2)}, u32[]{:S(2)}) collective-permute-start(f32[3,1,256,256]{3,2,1,0:T(8,128)S(1)} %shard_map.55), channel_id=1, source_target_pairs={{8,16},{16,8},{9,17},{17,9},{10,18},{18,10},{11,19},{19,11},{12,20... | collective-permute-start | bytes 2359304 | tf_op jit(solution)/shard_map/ppermute | solution.py:385
  10.4 3.9 %shard_map.51 = (f32[3,256,256]{2,1,0:T(8,128)S(1)}, f32[3,256,256]{2,1,0:T(8,128)S(1)}, bf16[5,256,256]{2,1,0:T(8,128)(2,1)S(1)}, bf16[5,256,256]{2,1,0:T(8,128...) custom-call(f32[8,2,256,256]{3,2,1,0:T(8,128)S(1)} %copy-done, ...), custom_call_target="tpu_custom_call" | custom-call | flops 1409286144 | bytes 12582912 | tf_op jit(solution)/shard_map/pallas_call | solution.py:331
  15.2 1.7 %collective-permute-done.1.outer_ref = f32[3,1,256,256]{3,2,1,0:T(8,128)S(1)} collective-permute-done((f32[3,1,256,256]{3,2,1,0:T(8,128)S(1)}, f32[3,1,256,256]{3,2,1,0:T(8,128)S(1)}, u32[]{:S(2)}, u32[]{:S(2)}) %collective-permute-start.1) | collective-permute-done | bytes 786464 | tf_op jit(solution)/shard_map/ppermute | solution.py:385
  16.9 1.3 %collective-permute-start.3 = (f32[256,256]{1,0:T(8,128)S(1)}, f32[256,256]{1,0:T(8,128)S(1)}, u32[]{:S(2)}, u32[]{:S(2)}) collective-permute-start(f32[256,256]{1,0:T(8,128)S(1)} %get-tuple-element.58), channel_id=1, source_target_pairs={{8,16},{9,17},{10,18},{11,19},{12,20},{13,21},{14,22},{15,23}} | collective-permute-start | bytes 786440 | tf_op jit(solution)/shard_map/ppermute | solution.py:455
  18.2 7.1 %collective-permute-done.4.outer_ref = f32[3,1,256,256]{3,2,1,0:T(8,128)S(1)} collective-permute-done((f32[3,1,256,256]{3,2,1,0:T(8,128)S(1)}, f32[3,1,256,256]{3,2,1,0:T(8,128)S(1)}, u32[]{:S(2)}, u32[]{:S(2)}) %collective-permute-start.4) | collective-permute-done | bytes 786464 | tf_op jit(solution)/shard_map/ppermute | solution.py:385
  25.4 1.3 %collective-permute-start.5 = (f32[256,256]{1,0:T(8,128)S(1)}, f32[256,256]{1,0:T(8,128)S(1)}, u32[]{:S(2)}, u32[]{:S(2)}) collective-permute-start(f32[256,256]{1,0:T(8,128)S(1)} %get-tuple-element.63), channel_id=1, source_target_pairs={{8,16},{9,17},{10,18},{11,19},{12,20},{13,21},{14,22},{15,23}} | collective-permute-start | bytes 786440 | tf_op jit(solution)/shard_map/ppermute | solution.py:455
  26.6 1.3 %shard_map.57 = (bf16[8,256,256]{2,1,0:T(8,128)(2,1)S(1)}, bf16[8,256,256]{2,1,0:T(8,128)(2,1)S(1)}) custom-call(f32[3,256,256]{2,1,0:T(8,128)S(1)} %get-tuple-element.49.open_ref, f32[3,1,256,256]{3,2,1,0:T(8,128)S(1)} %collective-permute-done.1.outer_ref, ...), custom_call_target="tpu_custom_call", output_to_operand_aliasing={{0}: (5, {}), {1}: (6, {})} | custom-call | flops 805306368 | bytes 4194304 | tf_op jit(solution)/shard_map/pallas_call | solution.py:331
  28.0 1.4 %shard_map.59 = (bf16[8,256,256]{2,1,0:T(8,128)(2,1)S(1)}, bf16[8,256,256]{2,1,0:T(8,128)(2,1)S(1)}) custom-call(f32[3,256,256]{2,1,0:T(8,128)S(1)} %get-tuple-element.59.open_ref, f32[3,1,256,256]{3,2,1,0:T(8,128)S(1)} %collective-permute-done.4.outer_ref, ...), custom_call_target="tpu_custom_call", output_to_operand_aliasing={{0}: (5, {}), {1}: (6, {})} | custom-call | flops 805306368 | bytes 4194304 | tf_op jit(solution)/shard_map/pallas_call | solution.py:331
  29.6 1.3 %collective-permute-start.6 = (f32[256,256]{1,0:T(8,128)S(1)}, f32[256,256]{1,0:T(8,128)S(1)}, u32[]{:S(2)}, u32[]{:S(2)}) collective-permute-start(f32[256,256]{1,0:T(8,128)S(1)} %shard_map.58), channel_id=1, source_target_pairs={{16,24},{17,25},{18,26},{19,27},{20,28},{21,29},{22,30},{23,31}} | collective-permute-start | bytes 786440 | tf_op jit(solution)/shard_map/ppermute | solution.py:457
  31.0 2.1 %collective-permute-done.5.carry_ref.refs_1_ = f32[256,256]{1,0:T(8,128)S(1)} collective-permute-done((f32[256,256]{1,0:T(8,128)S(1)}, f32[256,256]{1,0:T(8,128)S(1)}, u32[]{:S(2)}, u32[]{:S(2)}) %collective-permute-start.5) | collective-permute-done | bytes 262176 | tf_op jit(solution)/shard_map/ppermute | solution.py:455
  33.3 1.3 %collective-permute-start.7 = (f32[256,256]{1,0:T(8,128)S(1)}, f32[256,256]{1,0:T(8,128)S(1)}, u32[]{:S(2)}, u32[]{:S(2)}) collective-permute-start(f32[256,256]{1,0:T(8,128)S(1)} %shard_map.60), channel_id=1, source_target_pairs={{16,24},{17,25},{18,26},{19,27},{20,28},{21,29},{22,30},{23,31}} | collective-permute-start | bytes 786440 | tf_op jit(solution)/shard_map/ppermute | solution.py:457
  34.6 1.1 %collective-permute-done.7.refs_3_ = f32[256,256]{1,0:T(8,128)S(1)} collective-permute-done((f32[256,256]{1,0:T(8,128)S(1)}, f32[256,256]{1,0:T(8,128)S(1)}, u32[]{:S(2)}, u32[]{:S(2)}) %collective-permute-start.7) | collective-permute-done | bytes 262176 | tf_op jit(solution)/shard_map/ppermute | solution.py:457
  35.7 1.1 %shard_map.61 = (f32[3,2,256,256]{3,2,1,0:T(8,128)S(1)}, f32[4,3,32,256]{3,2,1,0:T(8,128)S(1)}, f32[4,3,32,256]{3,2,1,0:T(8,128)S(1)}, bf16[2,256,256]{2,1,0:T(8,128)(2,1)S(1)}, bf16[2,256,256]{2,1,0:T(8,128)(2,1)S(1)}) custom-call(f32[256,256]{1,0:T(8,128)S(1)} %collective-permute-done.3.carry_ref.refs_0_, ...), custom_call_target="tpu_custom_call" | custom-call | flops 603979776 | bytes 4718592 | tf_op jit(solution)/shard_map/pallas_call | solution.py:331
  36.8 1.6 %collective-permute-start.8 = (f32[4,3,32,256]{3,2,1,0:T(8,128)S(1)}, f32[4,3,32,256]{3,2,1,0:T(8,128)S(1)}, u32[]{:S(2)}, u32[]{:S(2)}) collective-permute-start(f32[4,3,32,256]{3,2,1,0:T(8,128)S(1)} %get-tuple-element.79), channel_id=1, source_target_pairs={{0,1},{1,0},{2,3},{3,2},{4,5},{5,4},{6,7},{7,6},{8,10},{9,11},{10,... | collective-permute-start | bytes 1179656 | tf_op jit(solution)/shard_map/ppermute | solution.py:508
  38.4 0.8 %shard_map.62 = (f32[3,2,256,256]{3,2,1,0:T(8,128)S(1)}, f32[4,3,32,256]{3,2,1,0:T(8,128)S(1)}, f32[4,3,32,256]{3,2,1,0:T(8,128)S(1)}) custom-call(bf16[2,256,256]{2,1,0:T(8,128)(2,1)S(1)} %get-tuple-element.74.refs_0_, bf16[2,256,256]{2,1,0:T(8,128)(2,1)S(1)} %get-tuple-element.75.refs_1_, ...), custom_call_target="tpu_custom_call" | custom-call | flops 603979776 | bytes 4718592 | tf_op jit(solution)/shard_map/pallas_call | solution.py:331
  40.5 1.6 %collective-permute-start.14 = (f32[4,2,32,256]{3,2,1,0:T(8,128)S(1)}, f32[4,2,32,256]{3,2,1,0:T(8,128)S(1)}, u32[]{:S(2)}, u32[]{:S(2)}) collective-permute-start(f32[4,2,32,256]{3,2,1,0:T(8,128)S(1)} %get-tuple-element.91), channel_id=1, source_target_pairs={{0,1},{1,0},{2,3},{3,2},{4,5},{5,4},{6,7},{7,6},{8,10},{9,11},{10,... | collective-permute-start | bytes 786440 | tf_op jit(solution)/shard_map/ppermute | solution.py:508
  42.0 2.6 %collective-permute-done.8.come_ref = f32[4,3,32,256]{3,2,1,0:T(8,128)S(1)} collective-permute-done((f32[4,3,32,256]{3,2,1,0:T(8,128)S(1)}, f32[4,3,32,256]{3,2,1,0:T(8,128)S(1)}, u32[]{:S(2)}, u32[]{:S(2)}) %collective-permute-start.8) | collective-permute-done | bytes 393248 | tf_op jit(solution)/shard_map/ppermute | solution.py:508
  44.7 1.6 %collective-permute-start.9 = (f32[2,3,32,256]{3,2,1,0:T(8,128)S(1)}, f32[2,3,32,256]{3,2,1,0:T(8,128)S(1)}, u32[]{:S(2)}, u32[]{:S(2)}) collective-permute-start(f32[2,3,32,256]{3,2,1,0:T(8,128)S(1)} %get-tuple-element.81), channel_id=1, source_target_pairs={{0,2},{1,3},{2,0},{3,1},{4,6},{5,7},{6,4},{7,5},{8,9},{9,8},{10,11... | collective-permute-start | bytes 589832 | tf_op jit(solution)/shard_map/ppermute | solution.py:508
  46.4 4.5 %collective-permute-done.11.come_ref = f32[4,3,32,256]{3,2,1,0:T(8,128)S(1)} collective-permute-done((f32[4,3,32,256]{3,2,1,0:T(8,128)S(1)}, f32[4,3,32,256]{3,2,1,0:T(8,128)S(1)}, u32[]{:S(2)}, u32[]{:S(2)}) %collective-permute-start.11) | collective-permute-done | bytes 393248 | tf_op jit(solution)/shard_map/ppermute | solution.py:508
  50.9 1.6 %collective-permute-start.12 = (f32[2,3,32,256]{3,2,1,0:T(8,128)S(1)}, f32[2,3,32,256]{3,2,1,0:T(8,128)S(1)}, u32[]{:S(2)}, u32[]{:S(2)}) collective-permute-start(f32[2,3,32,256]{3,2,1,0:T(8,128)S(1)} %get-tuple-element.87), channel_id=1, source_target_pairs={{0,2},{1,3},{2,0},{3,1},{4,6},{5,7},{6,4},{7,5},{8,9},{9,8},{10,11... | collective-permute-start | bytes 589832 | tf_op jit(solution)/shard_map/ppermute | solution.py:508
  52.6 3.3 %collective-permute-done.14.come_ref = f32[4,2,32,256]{3,2,1,0:T(8,128)S(1)} collective-permute-done((f32[4,2,32,256]{3,2,1,0:T(8,128)S(1)}, f32[4,2,32,256]{3,2,1,0:T(8,128)S(1)}, u32[]{:S(2)}, u32[]{:S(2)}) %collective-permute-start.14) | collective-permute-done | bytes 262176 | tf_op jit(solution)/shard_map/ppermute | solution.py:508
  56.0 1.6 %collective-permute-start.15 = (f32[2,2,32,256]{3,2,1,0:T(8,128)S(1)}, f32[2,2,32,256]{3,2,1,0:T(8,128)S(1)}, u32[]{:S(2)}, u32[]{:S(2)}) collective-permute-start(f32[2,2,32,256]{3,2,1,0:T(8,128)S(1)} %get-tuple-element.93), channel_id=1, source_target_pairs={{0,2},{1,3},{2,0},{3,1},{4,6},{5,7},{6,4},{7,5},{8,9},{9,8},{10,11... | collective-permute-start | bytes 393224 | tf_op jit(solution)/shard_map/ppermute | solution.py:508
  57.6 2.7 %collective-permute-start.10 = (f32[1,3,32,256]{3,2,1,0:T(8,128)S(1)}, f32[1,3,32,256]{3,2,1,0:T(8,128)S(1)}, u32[]{:S(2)}, u32[]{:S(2)}) collective-permute-start(f32[1,3,32,256]{3,2,1,0:T(8,128)S(1)} %get-tuple-element.83), channel_id=1, source_target_pairs={{0,4},{1,5},{2,6},{3,7},{4,0},{5,1},{6,2},{7,3},{8,12},{9,13},{10,... | collective-permute-start | bytes 294920 | tf_op jit(solution)/shard_map/ppermute | solution.py:508
  60.7 1.5 %collective-permute-done.15.come_ref = f32[2,2,32,256]{3,2,1,0:T(8,128)S(1)} collective-permute-done((f32[2,2,32,256]{3,2,1,0:T(8,128)S(1)}, f32[2,2,32,256]{3,2,1,0:T(8,128)S(1)}, u32[]{:S(2)}, u32[]{:S(2)}) %collective-permute-start.15) | collective-permute-done | bytes 131104 | tf_op jit(solution)/shard_map/ppermute | solution.py:508
  62.3 2.7 %collective-permute-start.16 = (f32[1,2,32,256]{3,2,1,0:T(8,128)S(1)}, f32[1,2,32,256]{3,2,1,0:T(8,128)S(1)}, u32[]{:S(2)}, u32[]{:S(2)}) collective-permute-start(f32[1,2,32,256]{3,2,1,0:T(8,128)S(1)} %get-tuple-element.95), channel_id=1, source_target_pairs={{0,4},{1,5},{2,6},{3,7},{4,0},{5,1},{6,2},{7,3},{8,12},{9,13},{10,... | collective-permute-start | bytes 196616 | tf_op jit(solution)/shard_map/ppermute | solution.py:508
  65.0 2.0 %shard_map.64 = f32[8,2,256,256]{3,2,1,0:T(8,128)} custom-call(f32[3,2,256,256]{3,2,1,0:T(8,128)S(1)} %get-tuple-element.73.refs_0_, f32[3,2,256,256]{3,2,1,0:T(8,128)S(1)} %get-tuple-element.76.refs_1_, f32[2,2,256,256]{3,2,1,0:T(8,128)S(1)} %get-tuple-element.77.refs_2_), custom_call_target="tpu_custom_call" | custom-call | bytes 8388608 | tf_op jit(solution)/shard_map/pallas_call | solution.py:331
  67.0 2.8 %collective-permute-done.16.refs_5_ = f32[1,2,32,256]{3,2,1,0:T(8,128)S(1)} collective-permute-done((f32[1,2,32,256]{3,2,1,0:T(8,128)S(1)}, f32[1,2,32,256]{3,2,1,0:T(8,128)S(1)}, u32[]{:S(2)}, u32[]{:S(2)}) %collective-permute-start.16) | collective-permute-done | bytes 65568 | tf_op jit(solution)/shard_map/ppermute | solution.py:508
  69.8 0.7 %shard_map.71 = f32[8,32,256]{2,1,0:T(8,128)} custom-call(f32[1,3,32,256]{3,2,1,0:T(8,128)S(1)} %get-tuple-element.82.refs_0_, f32[1,3,32,256]{3,2,1,0:T(8,128)S(1)} %collective-permute-done.10.refs_1_, f32[1,3,32,256]{3,2,1,0:T(8,128)S(1)} %get-tuple-element.88.refs_2_, f32[1,3,32,256]{3,2,1,0:T(8,128)S(1)} %collective-permute-done.13.refs_3_, ...), custom_call_target="tpu_custom_call" | custom-call | flops 65536 | bytes 786432 | tf_op jit(solution)/shard_map/pallas_call | solution.py:331
  (30 shorter events, 3.3 us)
Async XLA Ops:
  2.1 8.3 %collective-permute-start = (f32[3,2,256,256]{3,2,1,0:T(8,128)S(1)}, f32[3,2,256,256]{3,2,1,0:T(8,128)S(1)}, u32[]{:S(2)}, u32[]{:S(2)}) collective-permute-start(f32[3,2,256,256]{3,2,1,0:T(8,128)S(1)} %shard_map.50), channel_id=1, source_target_pairs={{0,8},{16,24},{8,0},{24,16},{1,9},{17,25},{9,1},{25,17},{2,10},{18... | collective-permute-start | bytes 4718600 | tf_op jit(solution)/shard_map/ppermute | solution.py:390
  3.3 7.1 %copy-start = (f32[8,2,256,256]{3,2,1,0:T(8,128)S(1)}, f32[8,2,256,256]{3,2,1,0:T(8,128)}, u32[]{:S(2)}) copy-start(f32[8,2,256,256]{3,2,1,0:T(8,128)} %raw_ref.5) | copy-start | bytes 12582916
  3.3 7.1 %copy-start.1 = (s32[2]{0:T(128)S(1)}, s32[2]{0:T(128)}, u32[]{:S(2)}) copy-start(s32[2]{0:T(128)} %refs_2_.1) | copy-start | bytes 28
  3.3 7.1 %copy-start.2 = (f32[2]{0:T(128)S(1)}, f32[2]{0:T(128)}, u32[]{:S(2)}) copy-start(f32[2]{0:T(128)} %refs_3_.1) | copy-start | bytes 28
  3.4 13.6 %collective-permute-start.1 = (f32[3,1,256,256]{3,2,1,0:T(8,128)S(1)}, f32[3,1,256,256]{3,2,1,0:T(8,128)S(1)}, u32[]{:S(2)}, u32[]{:S(2)}) collective-permute-start(f32[3,1,256,256]{3,2,1,0:T(8,128)S(1)} %shard_map.52), channel_id=1, source_target_pairs={{8,16},{16,8},{9,17},{17,9},{10,18},{18,10},{11,19},{19,11},{12,20... | collective-permute-start | bytes 2359304 | tf_op jit(solution)/shard_map/ppermute | solution.py:385
  6.7 18.6 %collective-permute-start.4 = (f32[3,1,256,256]{3,2,1,0:T(8,128)S(1)}, f32[3,1,256,256]{3,2,1,0:T(8,128)S(1)}, u32[]{:S(2)}, u32[]{:S(2)}) collective-permute-start(f32[3,1,256,256]{3,2,1,0:T(8,128)S(1)} %shard_map.55), channel_id=1, source_target_pairs={{8,16},{16,8},{9,17},{17,9},{10,18},{18,10},{11,19},{19,11},{12,20... | collective-permute-start | bytes 2359304 | tf_op jit(solution)/shard_map/ppermute | solution.py:385
  14.3 0.7 collective-permute-start.2
  16.9 12.4 %collective-permute-start.3 = (f32[256,256]{1,0:T(8,128)S(1)}, f32[256,256]{1,0:T(8,128)S(1)}, u32[]{:S(2)}, u32[]{:S(2)}) collective-permute-start(f32[256,256]{1,0:T(8,128)S(1)} %get-tuple-element.58), channel_id=1, source_target_pairs={{8,16},{9,17},{10,18},{11,19},{12,20},{13,21},{14,22},{15,23}} | collective-permute-start | bytes 786440 | tf_op jit(solution)/shard_map/ppermute | solution.py:455
  25.4 7.7 %collective-permute-start.5 = (f32[256,256]{1,0:T(8,128)S(1)}, f32[256,256]{1,0:T(8,128)S(1)}, u32[]{:S(2)}, u32[]{:S(2)}) collective-permute-start(f32[256,256]{1,0:T(8,128)S(1)} %get-tuple-element.63), channel_id=1, source_target_pairs={{8,16},{9,17},{10,18},{11,19},{12,20},{13,21},{14,22},{15,23}} | collective-permute-start | bytes 786440 | tf_op jit(solution)/shard_map/ppermute | solution.py:455
  29.6 5.0 %collective-permute-start.6 = (f32[256,256]{1,0:T(8,128)S(1)}, f32[256,256]{1,0:T(8,128)S(1)}, u32[]{:S(2)}, u32[]{:S(2)}) collective-permute-start(f32[256,256]{1,0:T(8,128)S(1)} %shard_map.58), channel_id=1, source_target_pairs={{16,24},{17,25},{18,26},{19,27},{20,28},{21,29},{22,30},{23,31}} | collective-permute-start | bytes 786440 | tf_op jit(solution)/shard_map/ppermute | solution.py:457
  33.3 2.4 %collective-permute-start.7 = (f32[256,256]{1,0:T(8,128)S(1)}, f32[256,256]{1,0:T(8,128)S(1)}, u32[]{:S(2)}, u32[]{:S(2)}) collective-permute-start(f32[256,256]{1,0:T(8,128)S(1)} %shard_map.60), channel_id=1, source_target_pairs={{16,24},{17,25},{18,26},{19,27},{20,28},{21,29},{22,30},{23,31}} | collective-permute-start | bytes 786440 | tf_op jit(solution)/shard_map/ppermute | solution.py:457
  36.8 7.8 %collective-permute-start.8 = (f32[4,3,32,256]{3,2,1,0:T(8,128)S(1)}, f32[4,3,32,256]{3,2,1,0:T(8,128)S(1)}, u32[]{:S(2)}, u32[]{:S(2)}) collective-permute-start(f32[4,3,32,256]{3,2,1,0:T(8,128)S(1)} %get-tuple-element.79), channel_id=1, source_target_pairs={{0,1},{1,0},{2,3},{3,2},{4,5},{5,4},{6,7},{7,6},{8,10},{9,11},{10,... | collective-permute-start | bytes 1179656 | tf_op jit(solution)/shard_map/ppermute | solution.py:508
  39.3 11.6 %collective-permute-start.11 = (f32[4,3,32,256]{3,2,1,0:T(8,128)S(1)}, f32[4,3,32,256]{3,2,1,0:T(8,128)S(1)}, u32[]{:S(2)}, u32[]{:S(2)}) collective-permute-start(f32[4,3,32,256]{3,2,1,0:T(8,128)S(1)} %get-tuple-element.85), channel_id=1, source_target_pairs={{0,1},{1,0},{2,3},{3,2},{4,5},{5,4},{6,7},{7,6},{8,10},{9,11},{10,... | collective-permute-start | bytes 1179656 | tf_op jit(solution)/shard_map/ppermute | solution.py:508
  40.5 15.5 %collective-permute-start.14 = (f32[4,2,32,256]{3,2,1,0:T(8,128)S(1)}, f32[4,2,32,256]{3,2,1,0:T(8,128)S(1)}, u32[]{:S(2)}, u32[]{:S(2)}) collective-permute-start(f32[4,2,32,256]{3,2,1,0:T(8,128)S(1)} %get-tuple-element.91), channel_id=1, source_target_pairs={{0,1},{1,0},{2,3},{3,2},{4,5},{5,4},{6,7},{7,6},{8,10},{9,11},{10,... | collective-permute-start | bytes 786440 | tf_op jit(solution)/shard_map/ppermute | solution.py:508
  44.7 12.9 %collective-permute-start.9 = (f32[2,3,32,256]{3,2,1,0:T(8,128)S(1)}, f32[2,3,32,256]{3,2,1,0:T(8,128)S(1)}, u32[]{:S(2)}, u32[]{:S(2)}) collective-permute-start(f32[2,3,32,256]{3,2,1,0:T(8,128)S(1)} %get-tuple-element.81), channel_id=1, source_target_pairs={{0,2},{1,3},{2,0},{3,1},{4,6},{5,7},{6,4},{7,5},{8,9},{9,8},{10,11... | collective-permute-start | bytes 589832 | tf_op jit(solution)/shard_map/ppermute | solution.py:508
  50.9 9.3 %collective-permute-start.12 = (f32[2,3,32,256]{3,2,1,0:T(8,128)S(1)}, f32[2,3,32,256]{3,2,1,0:T(8,128)S(1)}, u32[]{:S(2)}, u32[]{:S(2)}) collective-permute-start(f32[2,3,32,256]{3,2,1,0:T(8,128)S(1)} %get-tuple-element.87), channel_id=1, source_target_pairs={{0,2},{1,3},{2,0},{3,1},{4,6},{5,7},{6,4},{7,5},{8,9},{9,8},{10,11... | collective-permute-start | bytes 589832 | tf_op jit(solution)/shard_map/ppermute | solution.py:508
  56.0 6.3 %collective-permute-start.15 = (f32[2,2,32,256]{3,2,1,0:T(8,128)S(1)}, f32[2,2,32,256]{3,2,1,0:T(8,128)S(1)}, u32[]{:S(2)}, u32[]{:S(2)}) collective-permute-start(f32[2,2,32,256]{3,2,1,0:T(8,128)S(1)} %get-tuple-element.93), channel_id=1, source_target_pairs={{0,2},{1,3},{2,0},{3,1},{4,6},{5,7},{6,4},{7,5},{8,9},{9,8},{10,11... | collective-permute-start | bytes 393224 | tf_op jit(solution)/shard_map/ppermute | solution.py:508
  57.6 12.2 %collective-permute-start.10 = (f32[1,3,32,256]{3,2,1,0:T(8,128)S(1)}, f32[1,3,32,256]{3,2,1,0:T(8,128)S(1)}, u32[]{:S(2)}, u32[]{:S(2)}) collective-permute-start(f32[1,3,32,256]{3,2,1,0:T(8,128)S(1)} %get-tuple-element.83), channel_id=1, source_target_pairs={{0,4},{1,5},{2,6},{3,7},{4,0},{5,1},{6,2},{7,3},{8,12},{9,13},{10,... | collective-permute-start | bytes 294920 | tf_op jit(solution)/shard_map/ppermute | solution.py:508
  60.3 9.5 %collective-permute-start.13 = (f32[1,3,32,256]{3,2,1,0:T(8,128)S(1)}, f32[1,3,32,256]{3,2,1,0:T(8,128)S(1)}, u32[]{:S(2)}, u32[]{:S(2)}) collective-permute-start(f32[1,3,32,256]{3,2,1,0:T(8,128)S(1)} %get-tuple-element.89), channel_id=1, source_target_pairs={{0,4},{1,5},{2,6},{3,7},{4,0},{5,1},{6,2},{7,3},{8,12},{9,13},{10,... | collective-permute-start | bytes 294920 | tf_op jit(solution)/shard_map/ppermute | solution.py:508
  62.3 7.6 %collective-permute-start.16 = (f32[1,2,32,256]{3,2,1,0:T(8,128)S(1)}, f32[1,2,32,256]{3,2,1,0:T(8,128)S(1)}, u32[]{:S(2)}, u32[]{:S(2)}) collective-permute-start(f32[1,2,32,256]{3,2,1,0:T(8,128)S(1)} %get-tuple-element.95), channel_id=1, source_target_pairs={{0,4},{1,5},{2,6},{3,7},{4,0},{5,1},{6,2},{7,3},{8,12},{9,13},{10,... | collective-permute-start | bytes 196616 | tf_op jit(solution)/shard_map/ppermute | solution.py:508
where the time goes:
time: 70.9 us; the launch traced here: 70.6 us
  waiting for transfers between devices  26.9 us (38%)
  starting transfers between devices  26.2 us (37%)
  Pallas kernels  16.5 us (23%)
  between operations  0.91 us (1%)
    pallas_call x22, Pallas kernels, run(): pl.pallas_call(kernel, out_shape=out_shape, in_specs=in_specs, out_specs=...  16.5 us
    ppermute x9, waiting for transfers between devices, pipeline(): come = lax.ppermute(send, ('tm', 'cohort'), pairs)  14.8 us
    ppermute x9, starting transfers between devices, pipeline(): come = lax.ppermute(send, ('tm', 'cohort'), pairs)  14.5 us
    ppermute x2, waiting for transfers between devices, pipeline(): both = lax.ppermute(piece, 'tm', both_ways(hops))  8.84 us
    ppermute x2, starting transfers between devices, pipeline(): both = lax.ppermute(piece, 'tm', both_ways(hops))  5.83 us
    ppermute x2, starting transfers between devices, pipeline(): two = lax.ppermute(two, 'tm', [(target, target + 1)])  2.61 us
    ppermute x2, starting transfers between devices, pipeline(): one = lax.ppermute(handed, 'tm', [(source, target)])  2.56 us
    ppermute x2, waiting for transfers between devices, pipeline(): one = lax.ppermute(handed, 'tm', [(source, target)])  2.08 us
  transfers between devices with their start and end apart: 17, of which 9 were waited for; matrix products, arithmetic and copies ran while one was open for 0% of the time, Pallas kernels for 19%

commit v1 on v0

--- a/solution.py
+++ b/solution.py
@@ -175,26 +175,27 @@
             out_lo[group][...] = lo_refs[group][...]
 
 
-def closed(odd, open_ref, outer_ref, gate_ref, months):
+def closed(lines, odd, open_ref, outer_ref, gate_ref, months):
+    present = jnp.where(lax.axis_index("tm") == (lines - 1 if odd else 0), 0.0, 1.0).astype(f32)
     states = open_ref.shape[1]
     unit = unit_rows(states, states, 0)
     parts = []
     for k, month in enumerate(sides(months, odd)[0]):
         value = open_ref[k]
         for weight, at in outer_taps(months, odd, month):
-            value = value + weight * outer_ref[at, 0]
+            value = value + (weight * present) * outer_ref[at, 0]
         gate = gate_ref[k, 0:1, :]
         parts.append(split(jnp.where(gate > 0.0, value * gate, unit)))
     return parts
 
 
-def close_odd_kernel(open_ref, outer_ref, run_hi, run_lo, gate_ref, hi_ref, lo_ref, total_ref):
+def close_odd_kernel(lines, open_ref, outer_ref, run_hi, run_lo, gate_ref, hi_ref, lo_ref, total_ref):
     months = hi_ref.shape[0]
     begun = months - REACH
 
     @pl.when(lax.axis_index("tm") % 2 == 1)
     def _():
-        parts = closed(True, open_ref, outer_ref, gate_ref, months)
+        parts = closed(lines, True, open_ref, outer_ref, gate_ref, months)
         last = (run_hi[begun - 1], run_lo[begun - 1])
         for at in range(REACH):
             value = product(last, parts[at])
@@ -203,13 +204,13 @@
         total_ref[...] = value
 
 
-def close_even_kernel(open_ref, outer_ref, run_hi, run_lo, gate_ref, _hi, _lo, hi_ref, lo_ref):
+def close_even_kernel(lines, open_ref, outer_ref, run_hi, run_lo, gate_ref, _hi, _lo, hi_ref, lo_ref):
     months = hi_ref.shape[0]
     begun = months - REACH
 
     @pl.when(lax.axis_index("tm") % 2 == 0)
     def _():
-        parts = closed(False, open_ref, outer_ref, gate_ref, months)
+        parts = closed(lines, False, open_ref, outer_ref, gate_ref, months)
         last = parts[0]
         put(last, hi_ref, lo_ref, 0)
         for at in range(1, REACH):
@@ -378,16 +379,18 @@
     hops = [(i, i + 1) for i in range(1, lines - 1, 2)]
     cores = [(i, i + 1) for i in range(0, lines - 1, 2)]
     both_ways = lambda pairs: pairs + [(b, a) for a, b in pairs]
+    swapped = both_ways(cores)
+    round_trip = [(i, (i + 1) % lines) for i in range(lines)]
+    apart = [
+        (a * cohorts + c, b * cohorts + c) for a, b in both_ways(hops) for c in range(cohorts)
+    ] + [
+        (a * cohorts + c, a * cohorts + (c ^ 1)) for a in (0, lines - 1) for c in range(cohorts)
+    ]
     outer = []
     for group in range(groups):
         piece = cut(True, group, 1)
-        if True:
-            both = lax.ppermute(piece, "tm", both_ways(hops))
-            outer.append((both, both))
-        else:
-            down = lax.ppermute(piece, "tm", [(b, a) for a, b in hops])
-            outer.append((down, lax.ppermute(piece, "tm", hops)))
-    inner = lax.ppermute(cut(False, 0, groups), "tm", both_ways(cores))
+        outer.append(lax.ppermute(piece, ("tm", "cohort"), apart))
+    inner = lax.ppermute(cut(False, 0, groups), "tm", swapped)
 
     halves = [shaped((rest,) + block, bf16)] * groups
     early = call(
@@ -407,7 +410,7 @@
     )(transition, inner, entry, share)
     opened, run_hi, run_lo, gates = (early[k * groups : (k + 1) * groups] for k in range(4))
     first_total, parts = early[4 * groups :]
-    ahead = lax.ppermute(first_total, "tm", [(0, 1)])
+    ahead = lax.ppermute(first_total, "tm", swapped)
     led = call(
         lead_kernel,
         tuple(halves + halves),
@@ -423,22 +426,22 @@
     for group in range(groups):
         given = (run_hi[group], run_lo[group], gates[group])
         odd_hi, odd_lo, handed = call(
-            close_odd_kernel,
+            functools.partial(close_odd_kernel, lines),
             (all_months, all_months, shaped(block, f32)),
             [VMEM] * 5,
             (VMEM, VMEM, VMEM),
             flops * REACH,
             size * months * 2,
-        )(opened[group], outer[group][0], *given)
+        )(opened[group], outer[group], *given)
         hi_all, lo_all = call(
-            close_even_kernel,
+            functools.partial(close_even_kernel, lines),
             (all_months, all_months),
             [VMEM] * 7,
             (VMEM, VMEM),
             flops * months,
             size * months * 2,
             input_output_aliases={5: 0, 6: 1},
-        )(opened[group], outer[group][1], *given, odd_hi, odd_lo)
+        )(opened[group], outer[group], *given, odd_hi, odd_lo)
         hi.append(hi_all)
         lo.append(lo_all)
         first.append(jnp.zeros_like(handed) if not hops else None)
@@ -452,9 +455,10 @@
         for hop, (source, target) in enumerate(hops):
             if hop:
                 handed = cross(second[-1])
-            one = lax.ppermute(handed, "tm", [(source, target)])
+            way = round_trip if group == groups - 1 else [(source, target)]
+            one = lax.ppermute(handed, "tm", way)
             two = cross(one)
-            two = lax.ppermute(two, "tm", [(target, target + 1)])
+            two = lax.ppermute(two, "tm", swapped)
             if hop:
                 here = line // 2 == hop + 1
                 one, two = jnp.where(here, one, first[-1]), jnp.where(here, two, second[-1])

time: 70.9 us -> 67.6 us (0.953)
  the two profiles are of different devices: /device:TPU:2 before, /device:TPU:0 now
where the time goes in v1:
time: 67.6 us; the launch traced here: 67.4 us
  waiting for transfers between devices  28.5 us (42%)
  starting transfers between devices  20.4 us (30%)
  Pallas kernels  17.6 us (26%)
  between operations  0.85 us (1%)
    pallas_call x22, Pallas kernels, run(): pl.pallas_call(kernel, out_shape=out_shape, in_specs=in_specs, out_specs=...  17.6 us
    ppermute x9, starting transfers between devices, pipeline(): come = lax.ppermute(send, ('tm', 'cohort'), pairs)  15.1 us
    ppermute x9, waiting for transfers between devices, pipeline(): come = lax.ppermute(send, ('tm', 'cohort'), pairs)  14.1 us
    ppermute x2, waiting for transfers between devices, pipeline(): outer.append(lax.ppermute(piece, ('tm', 'cohort'), apart))  8.88 us
    ppermute x2, starting transfers between devices, pipeline(): outer.append(lax.ppermute(piece, ('tm', 'cohort'), apart))  2.84 us
    ppermute x2, waiting for transfers between devices, pipeline(): one = lax.ppermute(handed, 'tm', way)  2.12 us
    ppermute x1, waiting for transfers between devices, pipeline(): ahead = lax.ppermute(first_total, 'tm', swapped)  1.9 us
    ppermute x2, starting transfers between devices, pipeline(): one = lax.ppermute(handed, 'tm', way)  1.67 us
  transfers between devices with their start and end apart: 17, of which 10 were waited for; matrix products, arithmetic and copies ran while one was open for 0% of the time, Pallas kernels for 22%

profile of v1, /device:TPU:0, one launch (start us, length us, event | category | flops | bytes accessed | tf_op | source)
XLA Modules:
  0.0 67.4 jit_solution(11326342915092663378)
XLA Ops:
  0.6 1.4 %shard_map.50 = f32[3,2,256,256]{3,2,1,0:T(8,128)S(1)} custom-call(f32[8,2,256,256]{3,2,1,0:T(8,128)} %raw_ref.5), custom_call_target="tpu_custom_call" | custom-call | bytes 3145728 | tf_op jit(solution)/shard_map/pallas_call | solution.py:332
  2.1 0.6 collective-permute-start
  2.6 1.1 %shard_map.52 = f32[3,1,256,256]{3,2,1,0:T(8,128)S(1)} custom-call(f32[8,2,256,256]{3,2,1,0:T(8,128)} %raw_ref.5), custom_call_target="tpu_custom_call" | custom-call | bytes 1572864 | tf_op jit(solution)/shard_map/pallas_call | solution.py:332
  3.8 2.6 %collective-permute-start.1 = (f32[3,1,256,256]{3,2,1,0:T(8,128)S(1)}, f32[3,1,256,256]{3,2,1,0:T(8,128)S(1)}, u32[]{:S(2)}, u32[]{:S(2)}) collective-permute-start(f32[3,1,256,256]{3,2,1,0:T(8,128)S(1)} %shard_map.52), channel_id=1, source_target_pairs={{8,16},{9,17},{10,18},{11,19},{12,20},{13,21},{14,22},{15,23},{16,... | collective-permute-start | bytes 2359304 | tf_op jit(solution)/shard_map/ppermute | solution.py:392
  6.4 1.1 %shard_map.55 = f32[3,1,256,256]{3,2,1,0:T(8,128)S(1)} custom-call(f32[8,2,256,256]{3,2,1,0:T(8,128)} %raw_ref.5), custom_call_target="tpu_custom_call" | custom-call | bytes 1572864 | tf_op jit(solution)/shard_map/pallas_call | solution.py:332
  7.8 5.3 %shard_map.51 = (f32[3,256,256]{2,1,0:T(8,128)S(1)}, f32[3,256,256]{2,1,0:T(8,128)S(1)}, bf16[5,256,256]{2,1,0:T(8,128)(2,1)S(1)}, bf16[5,256,256]{2,1,0:T(8,128...) custom-call(f32[8,2,256,256]{3,2,1,0:T(8,128)S(1)} %copy-done, ...), custom_call_target="tpu_custom_call" | custom-call | flops 1409286144 | bytes 12582912 | tf_op jit(solution)/shard_map/pallas_call | solution.py:332
  13.2 1.9 %collective-permute-done.2.refs_0_ = f32[2,256,256]{2,1,0:T(8,128)S(1)} collective-permute-done((f32[2,256,256]{2,1,0:T(8,128)S(1)}, f32[2,256,256]{2,1,0:T(8,128)S(1)}, u32[]{:S(2)}, u32[]{:S(2)}) %collective-permute-start.2) | collective-permute-done | bytes 524320 | tf_op jit(solution)/shard_map/ppermute | solution.py:413
  15.3 1.1 %collective-permute-done.1.outer_ref = f32[3,1,256,256]{3,2,1,0:T(8,128)S(1)} collective-permute-done((f32[3,1,256,256]{3,2,1,0:T(8,128)S(1)}, f32[3,1,256,256]{3,2,1,0:T(8,128)S(1)}, u32[]{:S(2)}, u32[]{:S(2)}) %collective-permute-start.1) | collective-permute-done | bytes 786464 | tf_op jit(solution)/shard_map/ppermute | solution.py:392
  16.4 0.7 collective-permute-start.3
  17.1 7.8 %collective-permute-done.4.outer_ref = f32[3,1,256,256]{3,2,1,0:T(8,128)S(1)} collective-permute-done((f32[3,1,256,256]{3,2,1,0:T(8,128)S(1)}, f32[3,1,256,256]{3,2,1,0:T(8,128)S(1)}, u32[]{:S(2)}, u32[]{:S(2)}) %collective-permute-start.4) | collective-permute-done | bytes 786464 | tf_op jit(solution)/shard_map/ppermute | solution.py:392
  24.8 1.0 %collective-permute-start.5 = (f32[256,256]{1,0:T(8,128)S(1)}, f32[256,256]{1,0:T(8,128)S(1)}, u32[]{:S(2)}, u32[]{:S(2)}) collective-permute-start(f32[256,256]{1,0:T(8,128)S(1)} %get-tuple-element.63), channel_id=1, source_target_pairs={{0,8},{8,16},{16,24},{24,0},{1,9},{9,17},{17,25},{25,1},{2,10},{10... | collective-permute-start | bytes 786440 | tf_op jit(solution)/shard_map/ppermute | solution.py:459
  25.8 1.3 %shard_map.57 = (bf16[8,256,256]{2,1,0:T(8,128)(2,1)S(1)}, bf16[8,256,256]{2,1,0:T(8,128)(2,1)S(1)}) custom-call(f32[3,256,256]{2,1,0:T(8,128)S(1)} %get-tuple-element.49.open_ref, f32[3,1,256,256]{3,2,1,0:T(8,128)S(1)} %collective-permute-done.1.outer_ref, ...), custom_call_target="tpu_custom_call", output_to_operand_aliasing={{0}: (5, {}), {1}: (6, {})} | custom-call | flops 805306368 | bytes 4194304 | tf_op jit(solution)/shard_map/pallas_call | solution.py:332
  27.2 1.4 %shard_map.59 = (bf16[8,256,256]{2,1,0:T(8,128)(2,1)S(1)}, bf16[8,256,256]{2,1,0:T(8,128)(2,1)S(1)}) custom-call(f32[3,256,256]{2,1,0:T(8,128)S(1)} %get-tuple-element.59.open_ref, f32[3,1,256,256]{3,2,1,0:T(8,128)S(1)} %collective-permute-done.4.outer_ref, ...), custom_call_target="tpu_custom_call", output_to_operand_aliasing={{0}: (5, {}), {1}: (6, {})} | custom-call | flops 805306368 | bytes 4194304 | tf_op jit(solution)/shard_map/pallas_call | solution.py:332
  28.9 2.1 %collective-permute-done.5.carry_ref.refs_1_ = f32[256,256]{1,0:T(8,128)S(1)} collective-permute-done((f32[256,256]{1,0:T(8,128)S(1)}, f32[256,256]{1,0:T(8,128)S(1)}, u32[]{:S(2)}, u32[]{:S(2)}) %collective-permute-start.5) | collective-permute-done | bytes 262176 | tf_op jit(solution)/shard_map/ppermute | solution.py:459
  31.4 1.5 %collective-permute-done.7.refs_3_ = f32[256,256]{1,0:T(8,128)S(1)} collective-permute-done((f32[256,256]{1,0:T(8,128)S(1)}, f32[256,256]{1,0:T(8,128)S(1)}, u32[]{:S(2)}, u32[]{:S(2)}) %collective-permute-start.7) | collective-permute-done | bytes 262176 | tf_op jit(solution)/shard_map/ppermute | solution.py:461
  32.9 0.9 %shard_map.61 = (f32[3,2,256,256]{3,2,1,0:T(8,128)S(1)}, f32[4,3,32,256]{3,2,1,0:T(8,128)S(1)}, f32[4,3,32,256]{3,2,1,0:T(8,128)S(1)}, bf16[2,256,256]{2,1,0:T(8,128)(2,1)S(1)}, bf16[2,256,256]{2,1,0:T(8,128)(2,1)S(1)}) custom-call(f32[256,256]{1,0:T(8,128)S(1)} %collective-permute-done.3.carry_ref.refs_0_, ...), custom_call_target="tpu_custom_call" | custom-call | flops 603979776 | bytes 4718592 | tf_op jit(solution)/shard_map/pallas_call | solution.py:332
  33.8 1.7 %collective-permute-start.8 = (f32[4,3,32,256]{3,2,1,0:T(8,128)S(1)}, f32[4,3,32,256]{3,2,1,0:T(8,128)S(1)}, u32[]{:S(2)}, u32[]{:S(2)}) collective-permute-start(f32[4,3,32,256]{3,2,1,0:T(8,128)S(1)} %get-tuple-element.79), channel_id=1, source_target_pairs={{0,1},{1,0},{2,3},{3,2},{4,5},{5,4},{6,7},{7,6},{8,10},{9,11},{10,... | collective-permute-start | bytes 1179656 | tf_op jit(solution)/shard_map/ppermute | solution.py:512
  35.5 0.8 %shard_map.62 = (f32[3,2,256,256]{3,2,1,0:T(8,128)S(1)}, f32[4,3,32,256]{3,2,1,0:T(8,128)S(1)}, f32[4,3,32,256]{3,2,1,0:T(8,128)S(1)}) custom-call(bf16[2,256,256]{2,1,0:T(8,128)(2,1)S(1)} %get-tuple-element.74.refs_0_, bf16[2,256,256]{2,1,0:T(8,128)(2,1)S(1)} %get-tuple-element.75.refs_1_, ...), custom_call_target="tpu_custom_call" | custom-call | flops 603979776 | bytes 4718592 | tf_op jit(solution)/shard_map/pallas_call | solution.py:332
  36.8 0.6 shard_map.63
  37.4 1.7 %collective-permute-start.14 = (f32[4,2,32,256]{3,2,1,0:T(8,128)S(1)}, f32[4,2,32,256]{3,2,1,0:T(8,128)S(1)}, u32[]{:S(2)}, u32[]{:S(2)}) collective-permute-start(f32[4,2,32,256]{3,2,1,0:T(8,128)S(1)} %get-tuple-element.91), channel_id=1, source_target_pairs={{0,1},{1,0},{2,3},{3,2},{4,5},{5,4},{6,7},{7,6},{8,10},{9,11},{10,... | collective-permute-start | bytes 786440 | tf_op jit(solution)/shard_map/ppermute | solution.py:512
  39.1 2.5 %collective-permute-done.8.come_ref = f32[4,3,32,256]{3,2,1,0:T(8,128)S(1)} collective-permute-done((f32[4,3,32,256]{3,2,1,0:T(8,128)S(1)}, f32[4,3,32,256]{3,2,1,0:T(8,128)S(1)}, u32[]{:S(2)}, u32[]{:S(2)}) %collective-permute-start.8) | collective-permute-done | bytes 393248 | tf_op jit(solution)/shard_map/ppermute | solution.py:512
  41.7 1.7 %collective-permute-start.9 = (f32[2,3,32,256]{3,2,1,0:T(8,128)S(1)}, f32[2,3,32,256]{3,2,1,0:T(8,128)S(1)}, u32[]{:S(2)}, u32[]{:S(2)}) collective-permute-start(f32[2,3,32,256]{3,2,1,0:T(8,128)S(1)} %get-tuple-element.81), channel_id=1, source_target_pairs={{0,2},{1,3},{2,0},{3,1},{4,6},{5,7},{6,4},{7,5},{8,9},{9,8},{10,11... | collective-permute-start | bytes 589832 | tf_op jit(solution)/shard_map/ppermute | solution.py:512
  43.4 4.6 %collective-permute-done.11.come_ref = f32[4,3,32,256]{3,2,1,0:T(8,128)S(1)} collective-permute-done((f32[4,3,32,256]{3,2,1,0:T(8,128)S(1)}, f32[4,3,32,256]{3,2,1,0:T(8,128)S(1)}, u32[]{:S(2)}, u32[]{:S(2)}) %collective-permute-start.11) | collective-permute-done | bytes 393248 | tf_op jit(solution)/shard_map/ppermute | solution.py:512
  48.1 1.8 %collective-permute-start.12 = (f32[2,3,32,256]{3,2,1,0:T(8,128)S(1)}, f32[2,3,32,256]{3,2,1,0:T(8,128)S(1)}, u32[]{:S(2)}, u32[]{:S(2)}) collective-permute-start(f32[2,3,32,256]{3,2,1,0:T(8,128)S(1)} %get-tuple-element.87), channel_id=1, source_target_pairs={{0,2},{1,3},{2,0},{3,1},{4,6},{5,7},{6,4},{7,5},{8,9},{9,8},{10,11... | collective-permute-start | bytes 589832 | tf_op jit(solution)/shard_map/ppermute | solution.py:512
  49.8 3.1 %collective-permute-done.14.come_ref = f32[4,2,32,256]{3,2,1,0:T(8,128)S(1)} collective-permute-done((f32[4,2,32,256]{3,2,1,0:T(8,128)S(1)}, f32[4,2,32,256]{3,2,1,0:T(8,128)S(1)}, u32[]{:S(2)}, u32[]{:S(2)}) %collective-permute-start.14) | collective-permute-done | bytes 262176 | tf_op jit(solution)/shard_map/ppermute | solution.py:512
  53.0 1.7 %collective-permute-start.15 = (f32[2,2,32,256]{3,2,1,0:T(8,128)S(1)}, f32[2,2,32,256]{3,2,1,0:T(8,128)S(1)}, u32[]{:S(2)}, u32[]{:S(2)}) collective-permute-start(f32[2,2,32,256]{3,2,1,0:T(8,128)S(1)} %get-tuple-element.93), channel_id=1, source_target_pairs={{0,2},{1,3},{2,0},{3,1},{4,6},{5,7},{6,4},{7,5},{8,9},{9,8},{10,11... | collective-permute-start | bytes 393224 | tf_op jit(solution)/shard_map/ppermute | solution.py:512
  54.8 2.7 %collective-permute-start.10 = (f32[1,3,32,256]{3,2,1,0:T(8,128)S(1)}, f32[1,3,32,256]{3,2,1,0:T(8,128)S(1)}, u32[]{:S(2)}, u32[]{:S(2)}) collective-permute-start(f32[1,3,32,256]{3,2,1,0:T(8,128)S(1)} %get-tuple-element.83), channel_id=1, source_target_pairs={{0,4},{1,5},{2,6},{3,7},{4,0},{5,1},{6,2},{7,3},{8,12},{9,13},{10,... | collective-permute-start | bytes 294920 | tf_op jit(solution)/shard_map/ppermute | solution.py:512
  57.9 1.4 %collective-permute-done.15.come_ref = f32[2,2,32,256]{3,2,1,0:T(8,128)S(1)} collective-permute-done((f32[2,2,32,256]{3,2,1,0:T(8,128)S(1)}, f32[2,2,32,256]{3,2,1,0:T(8,128)S(1)}, u32[]{:S(2)}, u32[]{:S(2)}) %collective-permute-start.15) | collective-permute-done | bytes 131104 | tf_op jit(solution)/shard_map/ppermute | solution.py:512
  59.3 3.0 %collective-permute-start.16 = (f32[1,2,32,256]{3,2,1,0:T(8,128)S(1)}, f32[1,2,32,256]{3,2,1,0:T(8,128)S(1)}, u32[]{:S(2)}, u32[]{:S(2)}) collective-permute-start(f32[1,2,32,256]{3,2,1,0:T(8,128)S(1)} %get-tuple-element.95), channel_id=1, source_target_pairs={{0,4},{1,5},{2,6},{3,7},{4,0},{5,1},{6,2},{7,3},{8,12},{9,13},{10,... | collective-permute-start | bytes 196616 | tf_op jit(solution)/shard_map/ppermute | solution.py:512
  62.2 2.0 %shard_map.64 = f32[8,2,256,256]{3,2,1,0:T(8,128)} custom-call(f32[3,2,256,256]{3,2,1,0:T(8,128)S(1)} %get-tuple-element.73.refs_0_, f32[3,2,256,256]{3,2,1,0:T(8,128)S(1)} %get-tuple-element.76.refs_1_, f32[2,2,256,256]{3,2,1,0:T(8,128)S(1)} %get-tuple-element.77.refs_2_), custom_call_target="tpu_custom_call" | custom-call | bytes 8388608 | tf_op jit(solution)/shard_map/pallas_call | solution.py:332
  64.3 2.4 %collective-permute-done.16.refs_5_ = f32[1,2,32,256]{3,2,1,0:T(8,128)S(1)} collective-permute-done((f32[1,2,32,256]{3,2,1,0:T(8,128)S(1)}, f32[1,2,32,256]{3,2,1,0:T(8,128)S(1)}, u32[]{:S(2)}, u32[]{:S(2)}) %collective-permute-start.16) | collective-permute-done | bytes 65568 | tf_op jit(solution)/shard_map/ppermute | solution.py:512
  66.6 0.7 %shard_map.71 = f32[8,32,256]{2,1,0:T(8,128)} custom-call(f32[1,3,32,256]{3,2,1,0:T(8,128)S(1)} %get-tuple-element.82.refs_0_, f32[1,3,32,256]{3,2,1,0:T(8,128)S(1)} %collective-permute-done.10.refs_1_, f32[1,3,32,256]{3,2,1,0:T(8,128)S(1)} %get-tuple-element.88.refs_2_, f32[1,3,32,256]{3,2,1,0:T(8,128)S(1)} %collective-permute-done.13.refs_3_, ...), custom_call_target="tpu_custom_call" | custom-call | flops 65536 | bytes 786432 | tf_op jit(solution)/shard_map/pallas_call | solution.py:332
  (30 shorter events, 2.2 us)
Async XLA Ops:
  2.1 5.7 %collective-permute-start = (f32[3,2,256,256]{3,2,1,0:T(8,128)S(1)}, f32[3,2,256,256]{3,2,1,0:T(8,128)S(1)}, u32[]{:S(2)}, u32[]{:S(2)}) collective-permute-start(f32[3,2,256,256]{3,2,1,0:T(8,128)S(1)} %shard_map.50), channel_id=1, source_target_pairs={{0,8},{16,24},{8,0},{24,16},{1,9},{17,25},{9,1},{25,17},{2,10},{18... | collective-permute-start | bytes 4718600 | tf_op jit(solution)/shard_map/ppermute | solution.py:393
  3.8 4.0 %copy-start = (f32[8,2,256,256]{3,2,1,0:T(8,128)S(1)}, f32[8,2,256,256]{3,2,1,0:T(8,128)}, u32[]{:S(2)}) copy-start(f32[8,2,256,256]{3,2,1,0:T(8,128)} %raw_ref.5) | copy-start | bytes 12582916
  3.8 4.0 %copy-start.1 = (s32[2]{0:T(128)S(1)}, s32[2]{0:T(128)}, u32[]{:S(2)}) copy-start(s32[2]{0:T(128)} %refs_2_.1) | copy-start | bytes 28
  3.8 4.0 %copy-start.2 = (f32[2]{0:T(128)S(1)}, f32[2]{0:T(128)}, u32[]{:S(2)}) copy-start(f32[2]{0:T(128)} %refs_3_.1) | copy-start | bytes 28
  3.8 12.6 %collective-permute-start.1 = (f32[3,1,256,256]{3,2,1,0:T(8,128)S(1)}, f32[3,1,256,256]{3,2,1,0:T(8,128)S(1)}, u32[]{:S(2)}, u32[]{:S(2)}) collective-permute-start(f32[3,1,256,256]{3,2,1,0:T(8,128)S(1)} %shard_map.52), channel_id=1, source_target_pairs={{8,16},{9,17},{10,18},{11,19},{12,20},{13,21},{14,22},{15,23},{16,... | collective-permute-start | bytes 2359304 | tf_op jit(solution)/shard_map/ppermute | solution.py:392
  7.6 17.2 %collective-permute-start.4 = (f32[3,1,256,256]{3,2,1,0:T(8,128)S(1)}, f32[3,1,256,256]{3,2,1,0:T(8,128)S(1)}, u32[]{:S(2)}, u32[]{:S(2)}) collective-permute-start(f32[3,1,256,256]{3,2,1,0:T(8,128)S(1)} %shard_map.55), channel_id=1, source_target_pairs={{8,16},{9,17},{10,18},{11,19},{12,20},{13,21},{14,22},{15,23},{16,... | collective-permute-start | bytes 2359304 | tf_op jit(solution)/shard_map/ppermute | solution.py:392
  13.1 2.0 %collective-permute-start.2 = (f32[2,256,256]{2,1,0:T(8,128)S(1)}, f32[2,256,256]{2,1,0:T(8,128)S(1)}, u32[]{:S(2)}, u32[]{:S(2)}) collective-permute-start(f32[2,256,256]{2,1,0:T(8,128)S(1)} %get-tuple-element.50), channel_id=1, source_target_pairs={{0,8},{16,24},{8,0},{24,16},{1,9},{17,25},{9,1},{25,17},{2,10},{18... | collective-permute-start | bytes 1572872 | tf_op jit(solution)/shard_map/ppermute | solution.py:413
  16.4 12.1 %collective-permute-start.3 = (f32[256,256]{1,0:T(8,128)S(1)}, f32[256,256]{1,0:T(8,128)S(1)}, u32[]{:S(2)}, u32[]{:S(2)}) collective-permute-start(f32[256,256]{1,0:T(8,128)S(1)} %get-tuple-element.58), channel_id=1, source_target_pairs={{8,16},{9,17},{10,18},{11,19},{12,20},{13,21},{14,22},{15,23}} | collective-permute-start | bytes 786440 | tf_op jit(solution)/shard_map/ppermute | solution.py:459
  24.8 6.2 %collective-permute-start.5 = (f32[256,256]{1,0:T(8,128)S(1)}, f32[256,256]{1,0:T(8,128)S(1)}, u32[]{:S(2)}, u32[]{:S(2)}) collective-permute-start(f32[256,256]{1,0:T(8,128)S(1)} %get-tuple-element.63), channel_id=1, source_target_pairs={{0,8},{8,16},{16,24},{24,0},{1,9},{9,17},{17,25},{25,1},{2,10},{10... | collective-permute-start | bytes 786440 | tf_op jit(solution)/shard_map/ppermute | solution.py:459
  28.8 2.6 %collective-permute-start.6 = (f32[256,256]{1,0:T(8,128)S(1)}, f32[256,256]{1,0:T(8,128)S(1)}, u32[]{:S(2)}, u32[]{:S(2)}) collective-permute-start(f32[256,256]{1,0:T(8,128)S(1)} %shard_map.58), channel_id=1, source_target_pairs={{0,8},{16,24},{8,0},{24,16},{1,9},{17,25},{9,1},{25,17},{2,10},{18... | collective-permute-start | bytes 786440 | tf_op jit(solution)/shard_map/ppermute | solution.py:461
  31.3 1.6 %collective-permute-start.7 = (f32[256,256]{1,0:T(8,128)S(1)}, f32[256,256]{1,0:T(8,128)S(1)}, u32[]{:S(2)}, u32[]{:S(2)}) collective-permute-start(f32[256,256]{1,0:T(8,128)S(1)} %shard_map.60), channel_id=1, source_target_pairs={{0,8},{16,24},{8,0},{24,16},{1,9},{17,25},{9,1},{25,17},{2,10},{18... | collective-permute-start | bytes 786440 | tf_op jit(solution)/shard_map/ppermute | solution.py:461
  33.8 7.8 %collective-permute-start.8 = (f32[4,3,32,256]{3,2,1,0:T(8,128)S(1)}, f32[4,3,32,256]{3,2,1,0:T(8,128)S(1)}, u32[]{:S(2)}, u32[]{:S(2)}) collective-permute-start(f32[4,3,32,256]{3,2,1,0:T(8,128)S(1)} %get-tuple-element.79), channel_id=1, source_target_pairs={{0,1},{1,0},{2,3},{3,2},{4,5},{5,4},{6,7},{7,6},{8,10},{9,11},{10,... | collective-permute-start | bytes 1179656 | tf_op jit(solution)/shard_map/ppermute | solution.py:512
  36.3 11.7 %collective-permute-start.11 = (f32[4,3,32,256]{3,2,1,0:T(8,128)S(1)}, f32[4,3,32,256]{3,2,1,0:T(8,128)S(1)}, u32[]{:S(2)}, u32[]{:S(2)}) collective-permute-start(f32[4,3,32,256]{3,2,1,0:T(8,128)S(1)} %get-tuple-element.85), channel_id=1, source_target_pairs={{0,1},{1,0},{2,3},{3,2},{4,5},{5,4},{6,7},{7,6},{8,10},{9,11},{10,... | collective-permute-start | bytes 1179656 | tf_op jit(solution)/shard_map/ppermute | solution.py:512
  37.4 15.6 %collective-permute-start.14 = (f32[4,2,32,256]{3,2,1,0:T(8,128)S(1)}, f32[4,2,32,256]{3,2,1,0:T(8,128)S(1)}, u32[]{:S(2)}, u32[]{:S(2)}) collective-permute-start(f32[4,2,32,256]{3,2,1,0:T(8,128)S(1)} %get-tuple-element.91), channel_id=1, source_target_pairs={{0,1},{1,0},{2,3},{3,2},{4,5},{5,4},{6,7},{7,6},{8,10},{9,11},{10,... | collective-permute-start | bytes 786440 | tf_op jit(solution)/shard_map/ppermute | solution.py:512
  41.7 13.1 %collective-permute-start.9 = (f32[2,3,32,256]{3,2,1,0:T(8,128)S(1)}, f32[2,3,32,256]{3,2,1,0:T(8,128)S(1)}, u32[]{:S(2)}, u32[]{:S(2)}) collective-permute-start(f32[2,3,32,256]{3,2,1,0:T(8,128)S(1)} %get-tuple-element.81), channel_id=1, source_target_pairs={{0,2},{1,3},{2,0},{3,1},{4,6},{5,7},{6,4},{7,5},{8,9},{9,8},{10,11... | collective-permute-start | bytes 589832 | tf_op jit(solution)/shard_map/ppermute | solution.py:512
  48.1 9.4 %collective-permute-start.12 = (f32[2,3,32,256]{3,2,1,0:T(8,128)S(1)}, f32[2,3,32,256]{3,2,1,0:T(8,128)S(1)}, u32[]{:S(2)}, u32[]{:S(2)}) collective-permute-start(f32[2,3,32,256]{3,2,1,0:T(8,128)S(1)} %get-tuple-element.87), channel_id=1, source_target_pairs={{0,2},{1,3},{2,0},{3,1},{4,6},{5,7},{6,4},{7,5},{8,9},{9,8},{10,11... | collective-permute-start | bytes 589832 | tf_op jit(solution)/shard_map/ppermute | solution.py:512
  53.0 6.2 %collective-permute-start.15 = (f32[2,2,32,256]{3,2,1,0:T(8,128)S(1)}, f32[2,2,32,256]{3,2,1,0:T(8,128)S(1)}, u32[]{:S(2)}, u32[]{:S(2)}) collective-permute-start(f32[2,2,32,256]{3,2,1,0:T(8,128)S(1)} %get-tuple-element.93), channel_id=1, source_target_pairs={{0,2},{1,3},{2,0},{3,1},{4,6},{5,7},{6,4},{7,5},{8,9},{9,8},{10,11... | collective-permute-start | bytes 393224 | tf_op jit(solution)/shard_map/ppermute | solution.py:512
  54.8 11.8 %collective-permute-start.10 = (f32[1,3,32,256]{3,2,1,0:T(8,128)S(1)}, f32[1,3,32,256]{3,2,1,0:T(8,128)S(1)}, u32[]{:S(2)}, u32[]{:S(2)}) collective-permute-start(f32[1,3,32,256]{3,2,1,0:T(8,128)S(1)} %get-tuple-element.83), channel_id=1, source_target_pairs={{0,4},{1,5},{2,6},{3,7},{4,0},{5,1},{6,2},{7,3},{8,12},{9,13},{10,... | collective-permute-start | bytes 294920 | tf_op jit(solution)/shard_map/ppermute | solution.py:512
  57.5 9.2 %collective-permute-start.13 = (f32[1,3,32,256]{3,2,1,0:T(8,128)S(1)}, f32[1,3,32,256]{3,2,1,0:T(8,128)S(1)}, u32[]{:S(2)}, u32[]{:S(2)}) collective-permute-start(f32[1,3,32,256]{3,2,1,0:T(8,128)S(1)} %get-tuple-element.89), channel_id=1, source_target_pairs={{0,4},{1,5},{2,6},{3,7},{4,0},{5,1},{6,2},{7,3},{8,12},{9,13},{10,... | collective-permute-start | bytes 294920 | tf_op jit(solution)/shard_map/ppermute | solution.py:512
  59.3 7.4 %collective-permute-start.16 = (f32[1,2,32,256]{3,2,1,0:T(8,128)S(1)}, f32[1,2,32,256]{3,2,1,0:T(8,128)S(1)}, u32[]{:S(2)}, u32[]{:S(2)}) collective-permute-start(f32[1,2,32,256]{3,2,1,0:T(8,128)S(1)} %get-tuple-element.95), channel_id=1, source_target_pairs={{0,4},{1,5},{2,6},{3,7},{4,0},{5,1},{6,2},{7,3},{8,12},{9,13},{10,... | collective-permute-start | bytes 196616 | tf_op jit(solution)/shard_map/ppermute | solution.py:512

commit v2 on v1

--- a/solution.py
+++ b/solution.py
@@ -244,67 +244,86 @@
     return bits, other
 
 
-def apply_kernel(orders, groups, start, begin, *refs):
-    if begin:
-        firsts, seconds = refs[:groups], refs[groups : 2 * groups]
-        refs = refs[2 * groups :]
-    else:
-        carry_hi, carry_lo = refs[:2]
-        refs = refs[2:]
-    hi_refs, lo_refs = refs[:groups], refs[groups : 2 * groups]
-    share_ref, cum_ref, keep_ref, send_ref = refs[2 * groups : 2 * groups + 4]
-    refs = refs[2 * groups + 4 :]
-    if begin:
-        carry_hi, carry_lo = refs[:2]
-        refs = refs[2:]
-    (mix,) = refs
-    months, _, states = cum_ref.shape[:3]
+def taken_over(first_ref, second_ref, hi_ref, lo_ref):
+    line = lax.axis_index("tm")
+    states = hi_ref.shape[1]
+
+    @pl.when(line < 2)
+    def _():
+        put(split(unit_rows(states, states, 0)), hi_ref, lo_ref, 0)
+
+    if first_ref is not None:
+
+        @pl.when(jnp.logical_and(line >= 2, line % 2 == 0))
+        def _():
+            put(split(first_ref[...]), hi_ref, lo_ref, 0)
+
+    if second_ref is not None:
+
+        @pl.when(jnp.logical_and(line >= 2, line % 2 == 1))
+        def _():
+            put(split(second_ref[...]), hi_ref, lo_ref, 0)
+
+
+def ahead_kernel(first_ref, second_ref, hi_ref, lo_ref, cum_ref, carry_hi, carry_lo):
+    taken_over(first_ref, second_ref, carry_hi, carry_lo)
+    carry = (carry_hi[0], carry_lo[0])
+    for month in range(cum_ref.shape[0]):
+        cum_ref[month] = product(carry, (hi_ref[month], lo_ref[month]))
+
+
+def apply_kernel(orders, groups, start, core, *refs):
+    begin = core is not None
+    given, refs = (refs[:1], refs[1:]) if begin else (refs[:2], refs[2:])
+    other_refs, refs = refs[: groups - 1], refs[groups - 1 :]
+    hi_ref, lo_ref, share_ref = refs[:3]
+    refs = refs[3 + 5 * (core == 1) :]
+    cum_ref, keep_ref, send_ref = refs[:3]
+    carry_hi, carry_lo = refs[3:5] if begin else given
+    mix = refs[-1]
+    months = cum_ref.shape[0]
     line = lax.axis_index("tm")
     me = lax.axis_index("cohort")
     rows = keep_ref.shape[2]
     half = keep_ref.shape[0]
 
+    def run():
+        if begin:
+            handed = given[0]
+            taken_over(*((None, handed) if core else (handed, None)), carry_hi, carry_lo)
+        carry = (carry_hi[0], carry_lo[0])
+        for at in range(months):
+            value = product(carry, (hi_ref[start + at], lo_ref[start + at]))
+            cum_ref[at] = value
+            mixed = share_ref[groups - 1, 0:1, :] * value
+            for group, other in enumerate(other_refs):
+                mixed = mixed + share_ref[group, 0:1, :] * other[start + at]
+            mix[at] = mixed
+        for place in range(2 * half):
+            away = [place_of(order, place) for order in orders]
+            away = away[core] if begin else jnp.where(line % 2 == 0, away[0], away[1])
+            block = pl.ds(pl.multiple_of((me ^ away) * rows, 8), rows)
+            out = keep_ref if place < half else send_ref
+            for at in range(months):
+                out[place % half, at] = mix[at, block, :]
+
     if begin:
-
-        @pl.when(line < 2)
-        def _():
-            for group in range(groups):
-                put(split(unit_rows(states, states, 0)), carry_hi, carry_lo, group)
-
-        @pl.when(jnp.logical_and(line >= 2, line % 2 == 0))
-        def _():
-            for group in range(groups):
-                put(split(firsts[group][...]), carry_hi, carry_lo, group)
-
-        @pl.when(jnp.logical_and(line >= 2, line % 2 == 1))
-        def _():
-            for group in range(groups):
-                put(split(seconds[group][...]), carry_hi, carry_lo, group)
-
-    carry = [(carry_hi[group], carry_lo[group]) for group in range(groups)]
-    for at in range(months):
-        mixed = None
-        for group in range(groups):
-            month = (hi_refs[group][start + at], lo_refs[group][start + at])
-            value = product(carry[group], month)
-            cum_ref[at, group] = value
-            term = share_ref[group, 0:1, :] * value
-            mixed = term if mixed is None else mixed + term
-        mix[at] = mixed
-    for place in range(2 * half):
-        away = jnp.where(line % 2 == 0, place_of(orders[0], place), place_of(orders[1], place))
-        block = pl.ds(pl.multiple_of((me ^ away) * rows, 8), rows)
-        out = keep_ref if place < half else send_ref
-        for at in range(months):
-            out[place % half, at] = mix[at, block, :]
+        pl.when(line % 2 == core)(run)
+    else:
+        run()
 
 
 def store_kernel(*refs):
     *parts, out_ref, sems = refs
+    groups = out_ref.shape[1]
+    others, chunks = parts[: groups - 1], parts[groups - 1 :]
     copies, at = [], 0
-    for k, part in enumerate(parts):
+    for group, part in enumerate(others):
+        copies.append(pltpu.make_async_copy(part, out_ref.at[:, group], sems.at[group]))
+    for k, part in enumerate(chunks):
         months = part.shape[0]
-        copies.append(pltpu.make_async_copy(part, out_ref.at[pl.ds(at, months)], sems.at[k]))
+        target = out_ref.at[pl.ds(at, months), groups - 1]
+        copies.append(pltpu.make_async_copy(part, target, sems.at[groups - 1 + k]))
         at += months
     for copy in copies:
         copy.start()
@@ -467,30 +486,48 @@
     orders = halving_orders(cohorts)
     steps = len(orders[0])
     rows = states // cohorts
-    carry, cumulative, sums = None, [], []
+    others = [
+        call(
+            ahead_kernel,
+            shaped((months,) + block, f32),
+            [VMEM] * 4,
+            VMEM,
+            flops * months,
+            3 * size * months,
+            scratch_shapes=[pltpu.VMEM((1,) + block, bf16)] * 2,
+        )(first[group], second[group], hi[group], lo[group])
+        for group in range(groups - 1)
+    ]
+    known = (*others, hi[-1], lo[-1], parts)
+    cumulative, sums = list(others), []
     for chunk, (start, stop) in enumerate(month_chunks(months)):
         count = stop - start
         part = shaped((cohorts // 2, count, rows, states), f32)
-        begin = chunk == 0
-        outs = [shaped((count, groups) + block, f32), part, part]
-        if begin:
-            args = (*first, *second)
-            outs += [shaped((groups,) + block, bf16)] * 2
+        outs = (shaped((count,) + block, f32), part, part)
+
+        def apply(core, args, outs, aliases):
+            return call(
+                functools.partial(apply_kernel, orders, groups, start, core),
+                outs,
+                [VMEM] * len(args),
+                tuple([VMEM] * len(outs)),
+                flops * count,
+                size * groups * count * 3,
+                input_output_aliases=aliases,
+                scratch_shapes=[pltpu.VMEM((count,) + block, f32)],
+            )(*args)
+
+        if chunk == 0:
+            outs += (shaped((1,) + block, bf16),) * 2
+            made = apply(0, (first[-1], *known), outs, {})
+            args = (second[-1], *known, *made)
+            aliases = {len(args) - 5 + k: k for k in range(5)}
+            made = apply(1, args, outs, aliases)
+            carry = made[3:]
         else:
-            args = carry
-        made = call(
-            functools.partial(apply_kernel, orders, groups, start, begin),
-            tuple(outs),
-            [VMEM] * (len(args) + 2 * groups + 1),
-            tuple([VMEM] * len(outs)),
-            flops * groups * count,
-            size * groups * count * 3,
-            scratch_shapes=[pltpu.VMEM((count,) + block, f32)],
-        )(*args, *hi, *lo, parts)
+            made = apply(None, (*carry, *known), outs, {})
         cumulative.append(made[0])
         sums.append(made[1:3])
-        if begin:
-            carry = tuple(made[3:])
     cumulative = call(
         store_kernel,
         shaped(transition.shape, f32),

time: 67.6 us -> 67.8 us (level)
    ppermute x2, waiting for transfers between devices: 1.51 us -> 0.01 us  [pipeline(): two = lax.ppermute(two, 'tm', swapped)]
    ppermute x9, waiting for transfers between devices: 14.1 us -> 15.1 us  [pipeline(): come = lax.ppermute(send, ('tm', 'cohort'), pairs)]
    pallas_call x22 -> x24, Pallas kernels: 17.6 us -> 17.9 us  [run(): pl.pallas_call(kernel, out_shape=out_shape, in_specs=in_specs, out_specs=...]
  transfers between devices with their start and end apart: 17 -> 17, of which waited for: 10 -> 9; matrix products, arithmetic and copies ran while one was open for 0% -> 0% of each run, Pallas kernels for 22% -> 22%
where the time goes in v2:
time: 67.8 us; the launch traced here: 67.6 us
  waiting for transfers between devices  28 us (41%)
  starting transfers between devices  20.7 us (31%)
  Pallas kernels  17.9 us (26%)
  between operations  0.87 us (1%)
    pallas_call x24, Pallas kernels, run(): pl.pallas_call(kernel, out_shape=out_shape, in_specs=in_specs, out_specs=...  17.9 us
    ppermute x9, starting transfers between devices, pipeline(): come = lax.ppermute(send, ('tm', 'cohort'), pairs)  15.4 us
    ppermute x9, waiting for transfers between devices, pipeline(): come = lax.ppermute(send, ('tm', 'cohort'), pairs)  15.1 us
    ppermute x2, waiting for transfers between devices, pipeline(): outer.append(lax.ppermute(piece, ('tm', 'cohort'), apart))  8.88 us
    ppermute x2, starting transfers between devices, pipeline(): outer.append(lax.ppermute(piece, ('tm', 'cohort'), apart))  2.84 us
    ppermute x2, waiting for transfers between devices, pipeline(): one = lax.ppermute(handed, 'tm', way)  2.12 us
    ppermute x1, waiting for transfers between devices, pipeline(): ahead = lax.ppermute(first_total, 'tm', swapped)  1.9 us
    ppermute x2, starting transfers between devices, pipeline(): one = lax.ppermute(handed, 'tm', way)  1.66 us
  transfers between devices with their start and end apart: 17, of which 9 were waited for; matrix products, arithmetic and copies ran while one was open for 0% of the time, Pallas kernels for 22%

profile of v2, /device:TPU:0, one launch (start us, length us, event | category | flops | bytes accessed | tf_op | source)
XLA Modules:
  0.0 67.6 jit_solution(16941415085707703721)
XLA Ops:
  0.6 1.4 %shard_map.50 = f32[3,2,256,256]{3,2,1,0:T(8,128)S(1)} custom-call(f32[8,2,256,256]{3,2,1,0:T(8,128)} %raw_ref.5), custom_call_target="tpu_custom_call" | custom-call | bytes 3145728 | tf_op jit(solution)/shard_map/pallas_call | solution.py:351
  2.1 0.6 collective-permute-start
  2.6 1.1 %shard_map.52 = f32[3,1,256,256]{3,2,1,0:T(8,128)S(1)} custom-call(f32[8,2,256,256]{3,2,1,0:T(8,128)} %raw_ref.5), custom_call_target="tpu_custom_call" | custom-call | bytes 1572864 | tf_op jit(solution)/shard_map/pallas_call | solution.py:351
  3.8 2.6 %collective-permute-start.1 = (f32[3,1,256,256]{3,2,1,0:T(8,128)S(1)}, f32[3,1,256,256]{3,2,1,0:T(8,128)S(1)}, u32[]{:S(2)}, u32[]{:S(2)}) collective-permute-start(f32[3,1,256,256]{3,2,1,0:T(8,128)S(1)} %shard_map.52), channel_id=1, source_target_pairs={{8,16},{9,17},{10,18},{11,19},{12,20},{13,21},{14,22},{15,23},{16,... | collective-permute-start | bytes 2359304 | tf_op jit(solution)/shard_map/ppermute | solution.py:411
  6.4 1.1 %shard_map.58 = f32[3,1,256,256]{3,2,1,0:T(8,128)S(1)} custom-call(f32[8,2,256,256]{3,2,1,0:T(8,128)} %raw_ref.5), custom_call_target="tpu_custom_call" | custom-call | bytes 1572864 | tf_op jit(solution)/shard_map/pallas_call | solution.py:351
  7.8 5.3 %shard_map.51 = (f32[3,256,256]{2,1,0:T(8,128)S(1)}, f32[3,256,256]{2,1,0:T(8,128)S(1)}, bf16[5,256,256]{2,1,0:T(8,128)(2,1)S(1)}, bf16[5,256,256]{2,1,0:T(8,128...) custom-call(f32[8,2,256,256]{3,2,1,0:T(8,128)S(1)} %copy-done, ...), custom_call_target="tpu_custom_call" | custom-call | flops 1409286144 | bytes 12582912 | tf_op jit(solution)/shard_map/pallas_call | solution.py:351
  13.2 1.9 %collective-permute-done.2.refs_0_ = f32[2,256,256]{2,1,0:T(8,128)S(1)} collective-permute-done((f32[2,256,256]{2,1,0:T(8,128)S(1)}, f32[2,256,256]{2,1,0:T(8,128)S(1)}, u32[]{:S(2)}, u32[]{:S(2)}) %collective-permute-start.2) | collective-permute-done | bytes 524320 | tf_op jit(solution)/shard_map/ppermute | solution.py:432
  15.3 1.1 %collective-permute-done.1.outer_ref = f32[3,1,256,256]{3,2,1,0:T(8,128)S(1)} collective-permute-done((f32[3,1,256,256]{3,2,1,0:T(8,128)S(1)}, f32[3,1,256,256]{3,2,1,0:T(8,128)S(1)}, u32[]{:S(2)}, u32[]{:S(2)}) %collective-permute-start.1) | collective-permute-done | bytes 786464 | tf_op jit(solution)/shard_map/ppermute | solution.py:411
  16.4 0.7 collective-permute-start.3
  17.1 7.8 %collective-permute-done.5.outer_ref = f32[3,1,256,256]{3,2,1,0:T(8,128)S(1)} collective-permute-done((f32[3,1,256,256]{3,2,1,0:T(8,128)S(1)}, f32[3,1,256,256]{3,2,1,0:T(8,128)S(1)}, u32[]{:S(2)}, u32[]{:S(2)}) %collective-permute-start.5) | collective-permute-done | bytes 786464 | tf_op jit(solution)/shard_map/ppermute | solution.py:411
  24.8 1.0 %collective-permute-start.6 = (f32[256,256]{1,0:T(8,128)S(1)}, f32[256,256]{1,0:T(8,128)S(1)}, u32[]{:S(2)}, u32[]{:S(2)}) collective-permute-start(f32[256,256]{1,0:T(8,128)S(1)} %get-tuple-element.72), channel_id=1, source_target_pairs={{0,8},{8,16},{16,24},{24,0},{1,9},{9,17},{17,25},{25,1},{2,10},{10... | collective-permute-start | bytes 786440 | tf_op jit(solution)/shard_map/ppermute | solution.py:478
  25.8 1.3 %shard_map.55 = (bf16[8,256,256]{2,1,0:T(8,128)(2,1)S(1)}, bf16[8,256,256]{2,1,0:T(8,128)(2,1)S(1)}) custom-call(f32[3,256,256]{2,1,0:T(8,128)S(1)} %get-tuple-element.54.open_ref, f32[3,1,256,256]{3,2,1,0:T(8,128)S(1)} %collective-permute-done.1.outer_ref, ...), custom_call_target="tpu_custom_call", output_to_operand_aliasing={{0}: (5, {}), {1}: (6, {})} | custom-call | flops 805306368 | bytes 4194304 | tf_op jit(solution)/shard_map/pallas_call | solution.py:351
  27.5 1.4 %shard_map.60 = (bf16[8,256,256]{2,1,0:T(8,128)(2,1)S(1)}, bf16[8,256,256]{2,1,0:T(8,128)(2,1)S(1)}) custom-call(f32[3,256,256]{2,1,0:T(8,128)S(1)} %get-tuple-element.68.open_ref, f32[3,1,256,256]{3,2,1,0:T(8,128)S(1)} %collective-permute-done.5.outer_ref, ...), custom_call_target="tpu_custom_call", output_to_operand_aliasing={{0}: (5, {}), {1}: (6, {})} | custom-call | flops 805306368 | bytes 4194304 | tf_op jit(solution)/shard_map/pallas_call | solution.py:351
  28.9 2.1 %collective-permute-done.6.carry_ref.refs_0_ = f32[256,256]{1,0:T(8,128)S(1)} collective-permute-done((f32[256,256]{1,0:T(8,128)S(1)}, f32[256,256]{1,0:T(8,128)S(1)}, u32[]{:S(2)}, u32[]{:S(2)}) %collective-permute-start.6) | collective-permute-done | bytes 262176 | tf_op jit(solution)/shard_map/ppermute | solution.py:478
  31.4 1.0 %shard_map.57.refs_1_.refs_2_.refs_0_ = f32[8,256,256]{2,1,0:T(8,128)S(1)} custom-call(f32[256,256]{1,0:T(8,128)S(1)} %collective-permute-done.3.carry_ref.first_ref, f32[256,256]{1,0:T(8,128)S(1)} %collective-permute-done.4.second_ref, bf16[8,256,256]{2,1,0:T(8,128)(2,1)S(1)} %get-tuple-element.66.hi_ref, bf16[8,256,256]{2,1,0:T(8,128)(2,1)S(1)} %get-tuple-element.67.lo_ref), custom_call_target="tpu_custom_call" | custom-call | flops 805306368 | bytes 6291456 | tf_op jit(solution)/shard_map/pallas_call | solution.py:351
  32.4 0.6 shard_map.62
  33.1 0.5 shard_map.64
  33.6 1.7 %collective-permute-start.11 = (f32[4,3,32,256]{3,2,1,0:T(8,128)S(1)}, f32[4,3,32,256]{3,2,1,0:T(8,128)S(1)}, u32[]{:S(2)}, u32[]{:S(2)}) collective-permute-start(f32[4,3,32,256]{3,2,1,0:T(8,128)S(1)} %get-tuple-element.95), channel_id=1, source_target_pairs={{0,1},{1,0},{2,3},{3,2},{4,5},{5,4},{6,7},{7,6},{8,10},{9,11},{10,... | collective-permute-start | bytes 1179656 | tf_op jit(solution)/shard_map/ppermute | solution.py:549
  35.7 0.4 shard_map.65
  36.1 1.7 %collective-permute-start.14 = (f32[4,2,32,256]{3,2,1,0:T(8,128)S(1)}, f32[4,2,32,256]{3,2,1,0:T(8,128)S(1)}, u32[]{:S(2)}, u32[]{:S(2)}) collective-permute-start(f32[4,2,32,256]{3,2,1,0:T(8,128)S(1)} %get-tuple-element.101), channel_id=1, source_target_pairs={{0,1},{1,0},{2,3},{3,2},{4,5},{5,4},{6,7},{7,6},{8,10},{9,11},{10,... | collective-permute-start | bytes 786440 | tf_op jit(solution)/shard_map/ppermute | solution.py:549
  37.8 3.6 %collective-permute-done.11.come_ref = f32[4,3,32,256]{3,2,1,0:T(8,128)S(1)} collective-permute-done((f32[4,3,32,256]{3,2,1,0:T(8,128)S(1)}, f32[4,3,32,256]{3,2,1,0:T(8,128)S(1)}, u32[]{:S(2)}, u32[]{:S(2)}) %collective-permute-start.11) | collective-permute-done | bytes 393248 | tf_op jit(solution)/shard_map/ppermute | solution.py:549
  41.5 1.8 %collective-permute-start.12 = (f32[2,3,32,256]{3,2,1,0:T(8,128)S(1)}, f32[2,3,32,256]{3,2,1,0:T(8,128)S(1)}, u32[]{:S(2)}, u32[]{:S(2)}) collective-permute-start(f32[2,3,32,256]{3,2,1,0:T(8,128)S(1)} %get-tuple-element.97), channel_id=1, source_target_pairs={{0,2},{1,3},{2,0},{3,1},{4,6},{5,7},{6,4},{7,5},{8,9},{9,8},{10,11... | collective-permute-start | bytes 589832 | tf_op jit(solution)/shard_map/ppermute | solution.py:549
  43.2 4.2 %collective-permute-done.8.come_ref = f32[4,3,32,256]{3,2,1,0:T(8,128)S(1)} collective-permute-done((f32[4,3,32,256]{3,2,1,0:T(8,128)S(1)}, f32[4,3,32,256]{3,2,1,0:T(8,128)S(1)}, u32[]{:S(2)}, u32[]{:S(2)}) %collective-permute-start.8) | collective-permute-done | bytes 393248 | tf_op jit(solution)/shard_map/ppermute | solution.py:549
  47.5 1.8 %collective-permute-start.9 = (f32[2,3,32,256]{3,2,1,0:T(8,128)S(1)}, f32[2,3,32,256]{3,2,1,0:T(8,128)S(1)}, u32[]{:S(2)}, u32[]{:S(2)}) collective-permute-start(f32[2,3,32,256]{3,2,1,0:T(8,128)S(1)} %get-tuple-element.91), channel_id=1, source_target_pairs={{0,2},{1,3},{2,0},{3,1},{4,6},{5,7},{6,4},{7,5},{8,9},{9,8},{10,11... | collective-permute-start | bytes 589832 | tf_op jit(solution)/shard_map/ppermute | solution.py:549
  49.3 3.4 %collective-permute-done.14.come_ref = f32[4,2,32,256]{3,2,1,0:T(8,128)S(1)} collective-permute-done((f32[4,2,32,256]{3,2,1,0:T(8,128)S(1)}, f32[4,2,32,256]{3,2,1,0:T(8,128)S(1)}, u32[]{:S(2)}, u32[]{:S(2)}) %collective-permute-start.14) | collective-permute-done | bytes 262176 | tf_op jit(solution)/shard_map/ppermute | solution.py:549
  52.7 1.8 %collective-permute-start.15 = (f32[2,2,32,256]{3,2,1,0:T(8,128)S(1)}, f32[2,2,32,256]{3,2,1,0:T(8,128)S(1)}, u32[]{:S(2)}, u32[]{:S(2)}) collective-permute-start(f32[2,2,32,256]{3,2,1,0:T(8,128)S(1)} %get-tuple-element.103), channel_id=1, source_target_pairs={{0,2},{1,3},{2,0},{3,1},{4,6},{5,7},{6,4},{7,5},{8,9},{9,8},{10,11... | collective-permute-start | bytes 393224 | tf_op jit(solution)/shard_map/ppermute | solution.py:549
  54.5 2.7 %collective-permute-start.13 = (f32[1,3,32,256]{3,2,1,0:T(8,128)S(1)}, f32[1,3,32,256]{3,2,1,0:T(8,128)S(1)}, u32[]{:S(2)}, u32[]{:S(2)}) collective-permute-start(f32[1,3,32,256]{3,2,1,0:T(8,128)S(1)} %get-tuple-element.99), channel_id=1, source_target_pairs={{0,4},{1,5},{2,6},{3,7},{4,0},{5,1},{6,2},{7,3},{8,12},{9,13},{10,... | collective-permute-start | bytes 294920 | tf_op jit(solution)/shard_map/ppermute | solution.py:549
  57.6 0.8 %collective-permute-done.15.come_ref = f32[2,2,32,256]{3,2,1,0:T(8,128)S(1)} collective-permute-done((f32[2,2,32,256]{3,2,1,0:T(8,128)S(1)}, f32[2,2,32,256]{3,2,1,0:T(8,128)S(1)}, u32[]{:S(2)}, u32[]{:S(2)}) %collective-permute-start.15) | collective-permute-done | bytes 131104 | tf_op jit(solution)/shard_map/ppermute | solution.py:549
  58.4 3.3 %collective-permute-start.16 = (f32[1,2,32,256]{3,2,1,0:T(8,128)S(1)}, f32[1,2,32,256]{3,2,1,0:T(8,128)S(1)}, u32[]{:S(2)}, u32[]{:S(2)}) collective-permute-start(f32[1,2,32,256]{3,2,1,0:T(8,128)S(1)} %get-tuple-element.105), channel_id=1, source_target_pairs={{0,4},{1,5},{2,6},{3,7},{4,0},{5,1},{6,2},{7,3},{8,12},{9,13},{10,... | collective-permute-start | bytes 196616 | tf_op jit(solution)/shard_map/ppermute | solution.py:549
  61.7 2.0 %shard_map.66 = f32[8,2,256,256]{3,2,1,0:T(8,128)} custom-call(f32[8,256,256]{2,1,0:T(8,128)S(1)} %shard_map.57.refs_1_.refs_2_.refs_0_, f32[3,256,256]{2,1,0:T(8,128)S(1)} %get-tuple-element.83.refs_1_, f32[3,256,256]{2,1,0:T(8,128)S(1)} %get-tuple-element.86.refs_2_, f32[2,256,256]{2,1,0:T(8,128)S(1)} %get-tuple-element.87.refs_3_), custom_call_target="tpu_custom_call" | custom-call | bytes 8388608 | tf_op jit(solution)/shard_map/pallas_call | solution.py:351
  63.7 3.1 %collective-permute-done.16.refs_5_ = f32[1,2,32,256]{3,2,1,0:T(8,128)S(1)} collective-permute-done((f32[1,2,32,256]{3,2,1,0:T(8,128)S(1)}, f32[1,2,32,256]{3,2,1,0:T(8,128)S(1)}, u32[]{:S(2)}, u32[]{:S(2)}) %collective-permute-start.16) | collective-permute-done | bytes 65568 | tf_op jit(solution)/shard_map/ppermute | solution.py:549
  66.8 0.7 %shard_map.73 = f32[8,32,256]{2,1,0:T(8,128)} custom-call(f32[1,3,32,256]{3,2,1,0:T(8,128)S(1)} %get-tuple-element.92.refs_0_, f32[1,3,32,256]{3,2,1,0:T(8,128)S(1)} %collective-permute-done.10.refs_1_, f32[1,3,32,256]{3,2,1,0:T(8,128)S(1)} %get-tuple-element.98.refs_2_, f32[1,3,32,256]{3,2,1,0:T(8,128)S(1)} %collective-permute-done.13.refs_3_, ...), custom_call_target="tpu_custom_call" | custom-call | flops 65536 | bytes 786432 | tf_op jit(solution)/shard_map/pallas_call | solution.py:351
  (32 shorter events, 2.2 us)
Async XLA Ops:
  2.1 5.7 %collective-permute-start = (f32[3,2,256,256]{3,2,1,0:T(8,128)S(1)}, f32[3,2,256,256]{3,2,1,0:T(8,128)S(1)}, u32[]{:S(2)}, u32[]{:S(2)}) collective-permute-start(f32[3,2,256,256]{3,2,1,0:T(8,128)S(1)} %shard_map.50), channel_id=1, source_target_pairs={{0,8},{16,24},{8,0},{24,16},{1,9},{17,25},{9,1},{25,17},{2,10},{18... | collective-permute-start | bytes 4718600 | tf_op jit(solution)/shard_map/ppermute | solution.py:412
  3.8 4.0 %copy-start = (f32[8,2,256,256]{3,2,1,0:T(8,128)S(1)}, f32[8,2,256,256]{3,2,1,0:T(8,128)}, u32[]{:S(2)}) copy-start(f32[8,2,256,256]{3,2,1,0:T(8,128)} %raw_ref.5) | copy-start | bytes 12582916
  3.8 4.0 %copy-start.1 = (s32[2]{0:T(128)S(1)}, s32[2]{0:T(128)}, u32[]{:S(2)}) copy-start(s32[2]{0:T(128)} %refs_2_.1) | copy-start | bytes 28
  3.8 4.0 %copy-start.2 = (f32[2]{0:T(128)S(1)}, f32[2]{0:T(128)}, u32[]{:S(2)}) copy-start(f32[2]{0:T(128)} %refs_3_.1) | copy-start | bytes 28
  3.8 12.6 %collective-permute-start.1 = (f32[3,1,256,256]{3,2,1,0:T(8,128)S(1)}, f32[3,1,256,256]{3,2,1,0:T(8,128)S(1)}, u32[]{:S(2)}, u32[]{:S(2)}) collective-permute-start(f32[3,1,256,256]{3,2,1,0:T(8,128)S(1)} %shard_map.52), channel_id=1, source_target_pairs={{8,16},{9,17},{10,18},{11,19},{12,20},{13,21},{14,22},{15,23},{16,... | collective-permute-start | bytes 2359304 | tf_op jit(solution)/shard_map/ppermute | solution.py:411
  7.6 17.2 %collective-permute-start.5 = (f32[3,1,256,256]{3,2,1,0:T(8,128)S(1)}, f32[3,1,256,256]{3,2,1,0:T(8,128)S(1)}, u32[]{:S(2)}, u32[]{:S(2)}) collective-permute-start(f32[3,1,256,256]{3,2,1,0:T(8,128)S(1)} %shard_map.58), channel_id=1, source_target_pairs={{8,16},{9,17},{10,18},{11,19},{12,20},{13,21},{14,22},{15,23},{16,... | collective-permute-start | bytes 2359304 | tf_op jit(solution)/shard_map/ppermute | solution.py:411
  13.1 2.0 %collective-permute-start.2 = (f32[2,256,256]{2,1,0:T(8,128)S(1)}, f32[2,256,256]{2,1,0:T(8,128)S(1)}, u32[]{:S(2)}, u32[]{:S(2)}) collective-permute-start(f32[2,256,256]{2,1,0:T(8,128)S(1)} %get-tuple-element.55), channel_id=1, source_target_pairs={{0,8},{16,24},{8,0},{24,16},{1,9},{17,25},{9,1},{25,17},{2,10},{18... | collective-permute-start | bytes 1572872 | tf_op jit(solution)/shard_map/ppermute | solution.py:432
  16.4 10.8 %collective-permute-start.3 = (f32[256,256]{1,0:T(8,128)S(1)}, f32[256,256]{1,0:T(8,128)S(1)}, u32[]{:S(2)}, u32[]{:S(2)}) collective-permute-start(f32[256,256]{1,0:T(8,128)S(1)} %get-tuple-element.63), channel_id=1, source_target_pairs={{8,16},{9,17},{10,18},{11,19},{12,20},{13,21},{14,22},{15,23}} | collective-permute-start | bytes 786440 | tf_op jit(solution)/shard_map/ppermute | solution.py:478
  24.8 6.2 %collective-permute-start.6 = (f32[256,256]{1,0:T(8,128)S(1)}, f32[256,256]{1,0:T(8,128)S(1)}, u32[]{:S(2)}, u32[]{:S(2)}) collective-permute-start(f32[256,256]{1,0:T(8,128)S(1)} %get-tuple-element.72), channel_id=1, source_target_pairs={{0,8},{8,16},{16,24},{24,0},{1,9},{9,17},{17,25},{25,1},{2,10},{10... | collective-permute-start | bytes 786440 | tf_op jit(solution)/shard_map/ppermute | solution.py:478
  27.4 3.9 %collective-permute-start.4 = (f32[256,256]{1,0:T(8,128)S(1)}, f32[256,256]{1,0:T(8,128)S(1)}, u32[]{:S(2)}, u32[]{:S(2)}) collective-permute-start(f32[256,256]{1,0:T(8,128)S(1)} %shard_map.56), channel_id=1, source_target_pairs={{0,8},{16,24},{8,0},{24,16},{1,9},{17,25},{9,1},{25,17},{2,10},{18... | collective-permute-start | bytes 786440 | tf_op jit(solution)/shard_map/ppermute | solution.py:480
  31.3 1.7 %collective-permute-start.7 = (f32[256,256]{1,0:T(8,128)S(1)}, f32[256,256]{1,0:T(8,128)S(1)}, u32[]{:S(2)}, u32[]{:S(2)}) collective-permute-start(f32[256,256]{1,0:T(8,128)S(1)} %shard_map.61), channel_id=1, source_target_pairs={{0,8},{16,24},{8,0},{24,16},{1,9},{17,25},{9,1},{25,17},{2,10},{18... | collective-permute-start | bytes 786440 | tf_op jit(solution)/shard_map/ppermute | solution.py:480
  33.6 7.8 %collective-permute-start.11 = (f32[4,3,32,256]{3,2,1,0:T(8,128)S(1)}, f32[4,3,32,256]{3,2,1,0:T(8,128)S(1)}, u32[]{:S(2)}, u32[]{:S(2)}) collective-permute-start(f32[4,3,32,256]{3,2,1,0:T(8,128)S(1)} %get-tuple-element.95), channel_id=1, source_target_pairs={{0,1},{1,0},{2,3},{3,2},{4,5},{5,4},{6,7},{7,6},{8,10},{9,11},{10,... | collective-permute-start | bytes 1179656 | tf_op jit(solution)/shard_map/ppermute | solution.py:549
  35.3 12.2 %collective-permute-start.8 = (f32[4,3,32,256]{3,2,1,0:T(8,128)S(1)}, f32[4,3,32,256]{3,2,1,0:T(8,128)S(1)}, u32[]{:S(2)}, u32[]{:S(2)}) collective-permute-start(f32[4,3,32,256]{3,2,1,0:T(8,128)S(1)} %get-tuple-element.89), channel_id=1, source_target_pairs={{0,1},{1,0},{2,3},{3,2},{4,5},{5,4},{6,7},{7,6},{8,10},{9,11},{10,... | collective-permute-start | bytes 1179656 | tf_op jit(solution)/shard_map/ppermute | solution.py:549
  36.1 16.6 %collective-permute-start.14 = (f32[4,2,32,256]{3,2,1,0:T(8,128)S(1)}, f32[4,2,32,256]{3,2,1,0:T(8,128)S(1)}, u32[]{:S(2)}, u32[]{:S(2)}) collective-permute-start(f32[4,2,32,256]{3,2,1,0:T(8,128)S(1)} %get-tuple-element.101), channel_id=1, source_target_pairs={{0,1},{1,0},{2,3},{3,2},{4,5},{5,4},{6,7},{7,6},{8,10},{9,11},{10,... | collective-permute-start | bytes 786440 | tf_op jit(solution)/shard_map/ppermute | solution.py:549
  41.5 13.0 %collective-permute-start.12 = (f32[2,3,32,256]{3,2,1,0:T(8,128)S(1)}, f32[2,3,32,256]{3,2,1,0:T(8,128)S(1)}, u32[]{:S(2)}, u32[]{:S(2)}) collective-permute-start(f32[2,3,32,256]{3,2,1,0:T(8,128)S(1)} %get-tuple-element.97), channel_id=1, source_target_pairs={{0,2},{1,3},{2,0},{3,1},{4,6},{5,7},{6,4},{7,5},{8,9},{9,8},{10,11... | collective-permute-start | bytes 589832 | tf_op jit(solution)/shard_map/ppermute | solution.py:549
  47.5 9.6 %collective-permute-start.9 = (f32[2,3,32,256]{3,2,1,0:T(8,128)S(1)}, f32[2,3,32,256]{3,2,1,0:T(8,128)S(1)}, u32[]{:S(2)}, u32[]{:S(2)}) collective-permute-start(f32[2,3,32,256]{3,2,1,0:T(8,128)S(1)} %get-tuple-element.91), channel_id=1, source_target_pairs={{0,2},{1,3},{2,0},{3,1},{4,6},{5,7},{6,4},{7,5},{8,9},{9,8},{10,11... | collective-permute-start | bytes 589832 | tf_op jit(solution)/shard_map/ppermute | solution.py:549
  52.7 5.6 %collective-permute-start.15 = (f32[2,2,32,256]{3,2,1,0:T(8,128)S(1)}, f32[2,2,32,256]{3,2,1,0:T(8,128)S(1)}, u32[]{:S(2)}, u32[]{:S(2)}) collective-permute-start(f32[2,2,32,256]{3,2,1,0:T(8,128)S(1)} %get-tuple-element.103), channel_id=1, source_target_pairs={{0,2},{1,3},{2,0},{3,1},{4,6},{5,7},{6,4},{7,5},{8,9},{9,8},{10,11... | collective-permute-start | bytes 393224 | tf_op jit(solution)/shard_map/ppermute | solution.py:549
  54.5 12.3 %collective-permute-start.13 = (f32[1,3,32,256]{3,2,1,0:T(8,128)S(1)}, f32[1,3,32,256]{3,2,1,0:T(8,128)S(1)}, u32[]{:S(2)}, u32[]{:S(2)}) collective-permute-start(f32[1,3,32,256]{3,2,1,0:T(8,128)S(1)} %get-tuple-element.99), channel_id=1, source_target_pairs={{0,4},{1,5},{2,6},{3,7},{4,0},{5,1},{6,2},{7,3},{8,12},{9,13},{10,... | collective-permute-start | bytes 294920 | tf_op jit(solution)/shard_map/ppermute | solution.py:549
  57.2 9.7 %collective-permute-start.10 = (f32[1,3,32,256]{3,2,1,0:T(8,128)S(1)}, f32[1,3,32,256]{3,2,1,0:T(8,128)S(1)}, u32[]{:S(2)}, u32[]{:S(2)}) collective-permute-start(f32[1,3,32,256]{3,2,1,0:T(8,128)S(1)} %get-tuple-element.93), channel_id=1, source_target_pairs={{0,4},{1,5},{2,6},{3,7},{4,0},{5,1},{6,2},{7,3},{8,12},{9,13},{10,... | collective-permute-start | bytes 294920 | tf_op jit(solution)/shard_map/ppermute | solution.py:549
  58.4 8.5 %collective-permute-start.16 = (f32[1,2,32,256]{3,2,1,0:T(8,128)S(1)}, f32[1,2,32,256]{3,2,1,0:T(8,128)S(1)}, u32[]{:S(2)}, u32[]{:S(2)}) collective-permute-start(f32[1,2,32,256]{3,2,1,0:T(8,128)S(1)} %get-tuple-element.105), channel_id=1, source_target_pairs={{0,4},{1,5},{2,6},{3,7},{4,0},{5,1},{6,2},{7,3},{8,12},{9,13},{10,... | collective-permute-start | bytes 196616 | tf_op jit(solution)/shard_map/ppermute | solution.py:549
